TPU v7x, 512 devices: a whole 4x8x8 slice. The times are simulated.
512 devices in a mesh: block: 32 (over x, z), token: 16 (over y, core).
Axes of the slice: x: 4, y: 8, z: 8, core: 2. Of those that a mesh axis runs over, the one named last changes fastest.
Arguments:
- voxel_feats: bfloat16 [96, 524288], P(None, ('block', 'token')), may hold values from -6 to 6
- occupancy: int32 [524288], P(('block', 'token')), may hold values 0 or 1
- adjacency: int32 [2, 6, 1024], P(None, None, ('block', 'token')), may hold values from -1 to 31, as said below
- serial_pos: int32 [524288], P(('block', 'token')), may hold values from 0 to 16383, as said below
- conv_one: bfloat16 [7, 96, 96], replicated, may hold values from -0.25 to 0.25
- conv_two: bfloat16 [7, 96, 96], replicated, may hold values from -0.25 to 0.25
- gain_one: float32 [96], replicated, may hold values from 0.25 to 1.75
- gain_two: float32 [96], replicated, may hold values from 0.25 to 1.75
- gain_attn: float32 [96], replicated, may hold values from 0.25 to 1.75
- w_qkv: bfloat16 [144, 96], replicated, may hold values from -2 to 2
- w_out: bfloat16 [96, 48], replicated, may hold values from -4 to 4
- gain_mlp: float32 [96], replicated, may hold values from 0.25 to 1.75
- w_up: bfloat16 [384, 96], replicated, may hold values from -0.625 to 0.625
- w_down: bfloat16 [96, 384], replicated, may hold values from -0.3125 to 0.3125
Outputs:
- voxel_out: bfloat16 [96, 524288], P(None, ('block', 'token'))
Inputs may be any that keep to these rules, and one draw needn't show every extreme that they name: adjacency[0, f, g] is the segment of the neighbour of block g across face f, or -1 where there is none, and adjacency[1, f, g] is that neighbour's index among its device's 2 blocks (-1 with it). Neighbours lie in the same frame and at most 2 segments away; if block g' is the neighbour of g across face f, then g is the neighbour of g' across face f xor 1. At most 2 faces of one device have their neighbours on one other device. Within each group of rows k * 16384 to (k + 1) * 16384 - 1 (one segment of every frame), serial_pos is a permutation of 0 to 16383. At most 128 rows of one device take positions of any one device's range of 1024 positions, its own included.
All inputs are finite; a program needn't handle non-finite values. No bound on the sum of `occupancy` on one device may be relied on, other than what follows from the above.
Results may differ from a plain program's by a relative error of at most 0.04.
Values may be sent and summed in bfloat16 or wider, within the bound.
A program may use at most 64 MiB of HBM per device.

v0:
```python
import jax
import jax.numpy as jnp
from jax import lax
from jax.sharding import PartitionSpec as P

HEADS = 6
HD = 8
EDGE = 8
PATCH = 512
REACH = 2


EPS = 1e-05
FLIP = (1, 0, 3, 2, 5, 4)


def from_behind(block, axis, distance):
    devices = range(lax.axis_size(axis))
    route = [(i - distance, i) for i in devices if i - distance in devices]
    return lax.ppermute(block, axis, route)


def layer_norm(values, gain):
    center = values - jnp.mean(values, axis=0, keepdims=True)
    spread = jnp.mean(center * center, axis=0, keepdims=True)
    return center * lax.rsqrt(spread + EPS) * gain[:, None]


def face_layers(voxels):
    blocks_here = voxels.shape[1]
    face_list = [
        voxels[:, :, 0],
        voxels[:, :, -1],
        voxels[:, :, :, 0],
        voxels[:, :, :, -1],
        voxels[:, :, :, :, 0],
        voxels[:, :, :, :, -1],
    ]
    return jnp.stack(
        [
            jnp.transpose(face_layer, (1, 0, 2, 3)).reshape(blocks_here, -1)
            for face_layer in face_list
        ]
    )


def shifted_taps(voxels, halo_cube):
    return [
        voxels,
        jnp.concatenate([halo_cube[0][:, :, None], voxels[:, :, :-1]], axis=2),
        jnp.concatenate([voxels[:, :, 1:], halo_cube[1][:, :, None]], axis=2),
        jnp.concatenate([halo_cube[2][:, :, :, None], voxels[:, :, :, :-1]], axis=3),
        jnp.concatenate([voxels[:, :, :, 1:], halo_cube[3][:, :, :, None]], axis=3),
        jnp.concatenate([halo_cube[4][..., None], voxels[..., :-1]], axis=4),
        jnp.concatenate([voxels[..., 1:], halo_cube[5][..., None]], axis=4),
    ]


def neighbour_faces(faces, adjacency, segment):
    blocks_here = faces.shape[1]
    flat_size = faces.shape[2]
    owners = adjacency[0]
    indices = adjacency[1]
    flipped = jnp.array(FLIP, dtype=jnp.int32)
    present = owners >= 0
    gathered = []
    for offset in range(-REACH, REACH + 1):
        if offset == 0:
            gathered.append(faces)
        else:
            gathered.append(from_behind(faces, "block", -offset))
    stacked = jnp.stack(gathered).reshape(-1, flat_size)
    position = ((owners - segment + REACH) * 6 + flipped[:, None]) * blocks_here + indices
    picked = jnp.take(stacked, jnp.where(present, position, 0).reshape(-1), axis=0)
    picked = jnp.where(present.reshape(-1, 1), picked, jnp.zeros_like(picked))
    return picked.reshape(6, blocks_here, flat_size)


def cross_conv(signal, weight, adjacency, segment):
    channels, rows_here = signal.shape
    blocks_here = adjacency.shape[2]
    voxels = signal.reshape(channels, blocks_here, EDGE, EDGE, EDGE)
    halo_flat = neighbour_faces(face_layers(voxels), adjacency, segment)
    halo_cube = jnp.transpose(
        halo_flat.reshape(6, blocks_here, channels, EDGE, EDGE), (0, 2, 1, 3, 4)
    )
    taps_list = shifted_taps(voxels, halo_cube)
    accumulated = jnp.zeros((channels, rows_here), jnp.float32)
    for tap_index in range(7):
        accumulated = accumulated + jnp.dot(
            weight[tap_index],
            taps_list[tap_index].reshape(channels, rows_here),
            preferred_element_type=jnp.float32,
        )
    return accumulated


def per_device(
    voxel_feats,
    occupancy,
    adjacency,
    serial_pos,
    conv_one,
    conv_two,
    gain_one,
    gain_two,
    gain_attn,
    w_qkv,
    w_out,
    gain_mlp,
    w_up,
    w_down,
):
    channels, rows_here = voxel_feats.shape
    present = occupancy[None, :] > 0
    segment = lax.axis_index("block")
    signal = jnp.where(present, voxel_feats, jnp.zeros_like(voxel_feats))
    first_conv = cross_conv(signal, conv_one, adjacency, segment)
    middle = jnp.where(present, jax.nn.relu(layer_norm(first_conv, gain_one)), 0.0).astype(
        jnp.bfloat16
    )
    second_conv = cross_conv(middle, conv_two, adjacency, segment)
    block_out = jnp.where(
        present, jax.nn.relu(signal.astype(jnp.float32) + layer_norm(second_conv, gain_two)), 0.0
    ).astype(jnp.bfloat16)
    frames_here = lax.axis_size("token")
    capacity = 2 * rows_here // frames_here
    slots_total = frames_here * capacity
    target_dev = serial_pos // rows_here % frames_here
    target_row = serial_pos % rows_here
    member = (target_dev[:, None] == jnp.arange(frames_here, dtype=jnp.int32)[None, :]).astype(
        jnp.int32
    )
    rank_in = jnp.sum(jnp.cumsum(member, axis=0) * member, axis=1) - 1
    send_slot = target_dev * capacity + rank_in
    outgoing = jnp.zeros((channels, slots_total), jnp.bfloat16).at[:, send_slot].set(block_out)
    labels = jnp.stack(
        [
            jnp.full((slots_total,), rows_here, jnp.int32).at[send_slot].set(target_row),
            jnp.zeros((slots_total,), jnp.int32).at[send_slot].set(occupancy),
        ]
    )
    incoming, in_labels = (
        lax.all_to_all(outgoing, "token", split_axis=1, concat_axis=1, tiled=True),
        lax.all_to_all(labels, "token", split_axis=1, concat_axis=1, tiled=True),
    )
    serial = (
        jnp.zeros((channels, rows_here), jnp.bfloat16)
        .at[:, in_labels[0]]
        .set(incoming, mode="drop")
    )
    serial_live = jnp.zeros((rows_here,), jnp.int32).at[in_labels[0]].set(in_labels[1], mode="drop")
    normed = layer_norm(serial.astype(jnp.float32), gain_attn).astype(jnp.bfloat16)
    width_heads = HEADS * HD
    projected = jnp.dot(w_qkv, normed, preferred_element_type=jnp.float32)
    queries = projected[:width_heads].reshape(HEADS, HD, rows_here)
    keys_all = projected[width_heads : 2 * width_heads].reshape(HEADS, HD, rows_here)
    values_all = projected[2 * width_heads :].astype(jnp.bfloat16).reshape(HEADS, HD, rows_here)
    query_rows = min(512, PATCH)
    group_heads = 2
    patches_here = rows_here // PATCH
    query_blocks = PATCH // query_rows
    head_groups = HEADS // group_heads
    key_range = jnp.arange(PATCH, dtype=jnp.int32)

    def attend_step(step_index):
        head_group = step_index % head_groups
        remain = step_index // head_groups
        query_block = remain % query_blocks
        patch_index = remain // query_blocks
        key_start = patch_index * PATCH
        query_start = key_start + query_block * query_rows
        head_start = head_group * group_heads
        query_part = lax.dynamic_slice(
            queries, (head_start, 0, query_start), (group_heads, HD, query_rows)
        )
        key_part = lax.dynamic_slice(keys_all, (head_start, 0, key_start), (group_heads, HD, PATCH))
        value_part = lax.dynamic_slice(
            values_all, (head_start, 0, key_start), (group_heads, HD, PATCH)
        )
        live_keys = lax.dynamic_slice(serial_live, (key_start,), (PATCH,))
        scores = jnp.einsum(
            "hdq,hdk->hqk", query_part, key_part, precision=lax.Precision.HIGHEST
        ) * HD ** (-0.5)
        query_pos = query_block * query_rows + jnp.arange(query_rows, dtype=jnp.int32)
        allowed = (live_keys[None, :] > 0) | (query_pos[:, None] == key_range[None, :])
        scores = jnp.where(allowed[None], scores, -jnp.inf)
        largest = jnp.max(scores, axis=-1, keepdims=True)
        weights = jnp.exp(scores - largest)
        probability = (weights / jnp.sum(weights, axis=-1, keepdims=True)).astype(jnp.bfloat16)
        result = jnp.einsum(
            "hqk,hdk->hdq", probability, value_part, preferred_element_type=jnp.float32
        )
        return result.astype(jnp.bfloat16)

    total_steps = patches_here * query_blocks * head_groups
    pieces = lax.map(attend_step, jnp.arange(total_steps, dtype=jnp.int32))
    pieces = pieces.reshape(patches_here, query_blocks, head_groups, group_heads, HD, query_rows)
    heads_out = jnp.transpose(pieces, (2, 3, 4, 0, 1, 5)).reshape(width_heads, rows_here)
    attended = jnp.dot(w_out, heads_out, preferred_element_type=jnp.float32).astype(jnp.bfloat16)
    going_back = attended[:, jnp.minimum(in_labels[0], rows_here - 1)]
    returned_all = lax.all_to_all(going_back, "token", split_axis=1, concat_axis=1, tiled=True)
    returned = returned_all[:, send_slot]
    combined = block_out.astype(jnp.float32) + returned.astype(jnp.float32)
    tail_in = layer_norm(combined, gain_mlp).astype(jnp.bfloat16)
    hidden = jax.nn.gelu(jnp.dot(w_up, tail_in, preferred_element_type=jnp.float32)).astype(
        jnp.bfloat16
    )
    summed = combined + jnp.dot(w_down, hidden, preferred_element_type=jnp.float32)
    return jnp.where(present, summed, 0.0).astype(jnp.bfloat16)


def solution(mesh):
    in_specs = (
        P(None, ("block", "token")),
        P(("block", "token")),
        P(None, None, ("block", "token")),
        P(("block", "token")),
        P(),
        P(),
        P(),
        P(),
        P(),
        P(),
        P(),
        P(),
        P(),
        P(),
    )
    out_specs = P(None, ("block", "token"))
    return jax.shard_map(
        per_device, mesh=mesh, in_specs=in_specs, out_specs=out_specs, check_vma=False
    )
```

profile of v0, /device:TPU:1, one launch (start us, length us, event | category | flops | bytes accessed | tf_op | source)
XLA Modules:
  0.0 201.8 jit_solution(4519920368801786945)
XLA Ops:
  6.6 6.6 %collective-permute-start = (bf16[6,2,6144]{2,1,0:T(2,128)(2,1)S(1)}, bf16[6,2,6144]{2,1,0:T(2,128)(2,1)S(1)}, u32[]{:S(2)}, u32[]{:S(2)}) collective-permute-start(bf16[6,2,6144]{2,1,0:T(2,128)(2,1)S(1)} %constant_dynamic-update-slice_fusion), channel_id=1, source_target_pairs={{0,32},{16,48},{32,64},{48,80},{64,96},{80,112},{96,128},{112,144}... | collective-permute-start | bytes 442376 | tf_op jit(solution)/shard_map/ppermute | solution.py:20
  13.2 4.0 %collective-permute-start.1 = (bf16[6,2,6144]{2,1,0:T(2,128)(2,1)S(1)}, bf16[6,2,6144]{2,1,0:T(2,128)(2,1)S(1)}, u32[]{:S(2)}, u32[]{:S(2)}) collective-permute-start(bf16[6,2,6144]{2,1,0:T(2,128)(2,1)S(1)} %constant_dynamic-update-slice_fusion), channel_id=1, source_target_pairs={{0,16},{16,32},{32,48},{48,64},{64,80},{80,96},{96,112},{112,128},... | collective-permute-start | bytes 442376 | tf_op jit(solution)/shard_map/ppermute | solution.py:20
  17.2 1.3 collective-permute-start.2
  18.5 1.3 collective-permute-start.3
  19.9 4.5 %reduce-window.6 = s32[16,8,128]{2,1,0:T(8,128)S(1)} reduce-window(s32[16,8,128]{2,1,0:T(8,128)S(1)} %fusion.66, s32[]{:T(128)} %constant.198.clone.1), window={size=1x1x128 pad=0_0x0_0x127_0}, to_apply=%region_4.6 | reduce-window | flops 2080768 | bytes 131076 | tf_op jit(solution)/shard_map/reduce-window
  25.5 4.5 %scatter_custom_fusion.1 = s32[2048]{0:T(1024)S(1)} fusion(s32[1024]{0:T(1024)S(1)} %get-tuple-element.179, s32[1024]{0:T(1024)} %param.21, s32[]{:T(128)} %constant.198.clone.1), kind=kCustom, calls=%fused_computation.212 | custom fusion | bytes 8704 | tf_op jit(solution)/shard_map/scatter | solution.py:140
  29.9 4.3 %scatter_custom_fusion = s32[2048]{0:T(1024)S(1)} fusion(s32[1024]{0:T(1024)S(1)} %get-tuple-element.179, s32[1024]{0:T(1024)S(1)} %get-tuple-element.222, s32[]{:T(128)} %constant.207.clone.1), kind=kCustom, calls=%fused_computation.215 | custom fusion | bytes 8196 | tf_op jit(solution)/shard_map/scatter | solution.py:139
  34.9 8.3 %all-to-all-start = ((s32[2,16,128]{2,0,1:T(2,128)}), s32[2,16,128]{2,0,1:T(2,128)}, u32[]{:S(2)}, u32[]{:S(2)}) async-start(s32[2,16,128]{2,0,1:T(2,128)} %pad_add_fusion), calls=%async_computation | async-start | bytes 32768 | tf_op jit(solution)/shard_map/all_to_all | solution.py:145
  48.1 3.7 %reshape_reshape.6 = bf16[6,2,96,8,8]{4,3,2,1,0:T(8,128)(2,1)S(1)} reshape(bf16[12,6144]{1,0:T(8,128)(2,1)} %select_select_fusion.1) | data formatting | bytes 294912 | tf_op jit(solution)/shard_map/reshape;reshape | solution.py:85
  51.9 1.8 copy.164
  62.5 7.9 %collective-permute-start.4 = (bf16[6,2,6144]{2,1,0:T(2,128)(2,1)S(1)}, bf16[6,2,6144]{2,1,0:T(2,128)(2,1)S(1)}, u32[]{:S(2)}, u32[]{:S(2)}) collective-permute-start(bf16[6,2,6144]{2,1,0:T(2,128)(2,1)S(1)} %constant_dynamic-update-slice_fusion.6), channel_id=1, source_target_pairs={{0,32},{16,48},{32,64},{48,80},{64,96},{80,112},{96,128},{112,144}... | collective-permute-start | bytes 442376 | tf_op jit(solution)/shard_map/ppermute | solution.py:20
  70.4 3.1 %collective-permute-start.5 = (bf16[6,2,6144]{2,1,0:T(2,128)(2,1)S(1)}, bf16[6,2,6144]{2,1,0:T(2,128)(2,1)S(1)}, u32[]{:S(2)}, u32[]{:S(2)}) collective-permute-start(bf16[6,2,6144]{2,1,0:T(2,128)(2,1)S(1)} %constant_dynamic-update-slice_fusion.6), channel_id=1, source_target_pairs={{0,16},{16,32},{32,48},{48,64},{64,80},{80,96},{96,112},{112,128},... | collective-permute-start | bytes 442376 | tf_op jit(solution)/shard_map/ppermute | solution.py:20
  74.8 1.5 collective-permute-start.7
  78.5 3.3 %collective-permute-done.6 = bf16[6,2,6144]{2,1,0:T(2,128)(2,1)S(1)} collective-permute-done((bf16[6,2,6144]{2,1,0:T(2,128)(2,1)S(1)}, bf16[6,2,6144]{2,1,0:T(2,128)(2,1)S(1)}, u32[]{:S(2)}, u32[]{:S(2)}) %collective-permute-start.6) | collective-permute-done | bytes 147488 | tf_op jit(solution)/shard_map/ppermute | solution.py:20
  82.0 7.1 %collective-permute-done.7 = bf16[6,2,6144]{2,1,0:T(2,128)(2,1)S(1)} collective-permute-done((bf16[6,2,6144]{2,1,0:T(2,128)(2,1)S(1)}, bf16[6,2,6144]{2,1,0:T(2,128)(2,1)S(1)}, u32[]{:S(2)}, u32[]{:S(2)}) %collective-permute-start.7) | collective-permute-done | bytes 147488 | tf_op jit(solution)/shard_map/ppermute | solution.py:20
  90.3 2.9 %reshape_reshape.7 = bf16[6,2,96,8,8]{4,3,2,1,0:T(8,128)(2,1)S(1)} reshape(bf16[12,6144]{1,0:T(8,128)(2,1)S(1)} %select_select_fusion) | data formatting | bytes 294912 | tf_op jit(solution)/shard_map/reshape;reshape | solution.py:85
  100.0 3.5 %scatter_custom_fusion.2 = bf16[96,2048]{0,1:T(8,128)(2,1)S(1)} fusion(s32[1024]{0:T(1024)} %copy-done.20, bf16[1024,96]{1,0:T(8,128)(2,1)S(1)} %copy.185, bf16[]{:T(256)} %constant.199.clone.1), kind=kCustom, calls=%fused_computation.101 | custom fusion | bytes 393728 | tf_op jit(solution)/shard_map/scatter | solution.py:136
  104.4 8.4 %all-to-all-start.1 = ((bf16[96,16,128]{2,0,1:T(8,128)(2,1)}), bf16[96,16,128]{2,0,1:T(8,128)(2,1)S(1)}, u32[]{:S(2)}, u32[]{:S(2)}) async-start(bf16[96,16,128]{2,0,1:T(8,128)(2,1)} %copy.186), calls=%async_computation.1 | async-start | bytes 786432 | tf_op jit(solution)/shard_map/all_to_all | solution.py:144
  114.3 8.0 %scatter_custom_fusion.4 = s32[1024]{0:T(1024)S(1)} fusion(s32[2048]{0:T(1024)S(1)} %bitcast.364, s32[2048]{0:T(1024)S(1)} %bitcast.366, s32[]{:T(128)} %constant.198.clone.1), kind=kCustom, calls=%fused_computation.227 | custom fusion | bytes 4100 | tf_op jit(solution)/shard_map/scatter | solution.py:152
  122.4 5.0 %all-to-all-done.1 = bf16[96,16,128]{2,0,1:T(8,128)(2,1)S(1)} async-done(((bf16[96,16,128]{2,0,1:T(8,128)(2,1)}), bf16[96,16,128]{2,0,1:T(8,128)(2,1)S(1)}, u32[]{:S(2)}, u32[]{:S(2)}) %all-to-all-start.1) | async-done | bytes 393248 | tf_op jit(solution)/shard_map/all_to_all | solution.py:144
  127.6 6.0 %scatter_custom_fusion.3 = bf16[96,1024]{0,1:T(8,128)(2,1)S(1)} fusion(s32[2048]{0:T(1024)S(1)} %bitcast.365, bf16[2048,96]{1,0:T(8,128)(2,1)S(1)} %copy.189, bf16[]{:T(256)} %constant.199.clone.1), kind=kCustom, calls=%fused_computation.122 | custom fusion | bytes 196610 | tf_op jit(solution)/shard_map/scatter | solution.py:150
  134.8 37.3 %while.14 = (s32[]{:T(128)}, bf16[6,2,8,512]{3,2,1,0:T(8,128)(2,1)S(1)}, s32[6]{0:T(128)S(1)}, bf16[6,8,1024]{2,1,0:T(8,128)(2,1)S(1)}, s32[1024]{0:T(1024)S(1)}...) while((s32[]{:T(128)}, ...), condition=%wide.region_17.19_spmd.clone, body=%wide.region_14.18_spmd.clone.sunk | while | flops 63973908 | bytes 7189896 | solution.py:197
  137.4 1.8 fusion.151
  143.6 1.8 fusion.151
  149.8 1.8 fusion.151
  156.0 1.8 fusion.151
  162.2 1.8 fusion.151
  168.4 1.8 fusion.151
  172.7 6.2 %gather_fusion = bf16[2048,96]{1,0:T(8,128)(2,1)S(1)} fusion(bf16[96,1024]{0,1:T(8,128)(2,1)S(1)} %copy.191, s32[2048]{0:T(1024)S(1)} %broadcast_clamp_fusion), kind=kCustom, calls=%fused_computation.2 | custom fusion | bytes 794624 | tf_op jit(solution)/shard_map/gather | solution.py:201
  179.1 17.2 %all_to_all.30 = bf16[96,16,128]{2,0,1:T(8,128)(2,1)S(1)} all-to-all(bf16[96,16,128]{2,0,1:T(8,128)(2,1)S(1)} %copy.192), channel_id=1, replica_groups=mesh['block'=32,'token'=16] {'token'}, dimensions={1} | all-to-all | bytes 786432 | tf_op jit(solution)/shard_map/all_to_all | solution.py:202
  196.6 3.2 %gather_fusion.1 = bf16[1024,96]{1,0:T(8,128)(2,1)S(1)} fusion(bf16[96,2048]{0,1:T(8,128)(2,1)S(1)} %bitcast.333, s32[1024]{0:T(1024)S(1)} %copy-done.12), kind=kCustom, calls=%fused_computation.3 | custom fusion | bytes 397312 | tf_op jit(solution)/shard_map/gather | solution.py:203
  200.2 1.6 fusion.34
  (250 shorter events, 52.7 us)
Async XLA Ops:
  0.0 200.2 %copy-start = (bf16[96,384]{1,0:T(8,128)(2,1)S(1)}, bf16[96,384]{1,0:T(8,128)(2,1)}, u32[]{:S(2)}) copy-start(bf16[96,384]{1,0:T(8,128)(2,1)} %param.33) | copy-start | bytes 221188
  3.5 16.3 %copy-start.19 = (s32[1024]{0:T(1024)S(1)}, s32[1024]{0:T(1024)}, u32[]{:S(2)}) copy-start(s32[1024]{0:T(1024)} %param.23) | copy-start | bytes 12292
  6.0 38.9 %copy-start.22 = (s32[2,6,2]{1,2,0:T(2,128)S(1)}, s32[2,6,2]{1,2,0:T(2,128)}, u32[]{:S(2)}) copy-start(s32[2,6,2]{1,2,0:T(2,128)} %param.22) | copy-start | bytes 292
  6.0 39.5 %copy-start.24 = (s32[6]{0:T(128)S(1)}, s32[6]{0:T(128)}, u32[]{:S(2)}) copy-start(s32[6]{0:T(128)} %constant.220.clone) | copy-start | bytes 76
  6.6 39.2 %collective-permute-start = (bf16[6,2,6144]{2,1,0:T(2,128)(2,1)S(1)}, bf16[6,2,6144]{2,1,0:T(2,128)(2,1)S(1)}, u32[]{:S(2)}, u32[]{:S(2)}) collective-permute-start(bf16[6,2,6144]{2,1,0:T(2,128)(2,1)S(1)} %constant_dynamic-update-slice_fusion), channel_id=1, source_target_pairs={{0,32},{16,48},{32,64},{48,80},{64,96},{80,112},{96,128},{112,144}... | collective-permute-start | bytes 442376 | tf_op jit(solution)/shard_map/ppermute | solution.py:20
  13.2 32.6 %collective-permute-start.1 = (bf16[6,2,6144]{2,1,0:T(2,128)(2,1)S(1)}, bf16[6,2,6144]{2,1,0:T(2,128)(2,1)S(1)}, u32[]{:S(2)}, u32[]{:S(2)}) collective-permute-start(bf16[6,2,6144]{2,1,0:T(2,128)(2,1)S(1)} %constant_dynamic-update-slice_fusion), channel_id=1, source_target_pairs={{0,16},{16,32},{32,48},{48,64},{64,80},{80,96},{96,112},{112,128},... | collective-permute-start | bytes 442376 | tf_op jit(solution)/shard_map/ppermute | solution.py:20
  17.2 28.9 %collective-permute-start.2 = (bf16[6,2,6144]{2,1,0:T(2,128)(2,1)S(1)}, bf16[6,2,6144]{2,1,0:T(2,128)(2,1)S(1)}, u32[]{:S(2)}, u32[]{:S(2)}) collective-permute-start(bf16[6,2,6144]{2,1,0:T(2,128)(2,1)S(1)} %constant_dynamic-update-slice_fusion), channel_id=1, source_target_pairs={{16,0},{32,16},{48,32},{64,48},{80,64},{96,80},{112,96},{128,112},... | collective-permute-start | bytes 442376 | tf_op jit(solution)/shard_map/ppermute | solution.py:20
  18.5 27.7 %collective-permute-start.3 = (bf16[6,2,6144]{2,1,0:T(2,128)(2,1)S(1)}, bf16[6,2,6144]{2,1,0:T(2,128)(2,1)S(1)}, u32[]{:S(2)}, u32[]{:S(2)}) collective-permute-start(bf16[6,2,6144]{2,1,0:T(2,128)(2,1)S(1)} %constant_dynamic-update-slice_fusion), channel_id=1, source_target_pairs={{32,0},{48,16},{64,32},{80,48},{96,64},{112,80},{128,96},{144,112}... | collective-permute-start | bytes 442376 | tf_op jit(solution)/shard_map/ppermute | solution.py:20
  25.5 19.5 %copy-start.20 = (s32[1024]{0:T(1024)}, s32[1024]{0:T(1024)S(1)}, u32[]{:S(2)}) copy-start(s32[1024]{0:T(1024)S(1)} %get-tuple-element.179) | copy-start | bytes 12292
  34.9 69.5 %all-to-all-start = ((s32[2,16,128]{2,0,1:T(2,128)}), s32[2,16,128]{2,0,1:T(2,128)}, u32[]{:S(2)}, u32[]{:S(2)}) async-start(s32[2,16,128]{2,0,1:T(2,128)} %pad_add_fusion), calls=%async_computation | async-start | bytes 32768 | tf_op jit(solution)/shard_map/all_to_all | solution.py:145
  45.2 2.2 %copy-start.15 = (pred[12]{0:T(512)(128)(4,1)}, pred[12]{0:T(512)(128)(4,1)S(1)}, u32[]{:S(2)}) copy-start(pred[12]{0:T(512)(128)(4,1)S(1)} %ge.18) | copy-start | bytes 40
  45.7 1.6 copy-start.17
  45.7 1.6 copy-start.14
  51.9 4.0 %copy-start.6 = (bf16[7,96,96]{2,1,0:T(8,128)(2,1)S(1)}, bf16[7,96,96]{2,1,0:T(8,128)(2,1)}, u32[]{:S(2)}) copy-start(bf16[7,96,96]{2,1,0:T(8,128)(2,1)} %param.24) | copy-start | bytes 387076
  54.6 2.0 copy-start.4
  62.5 15.7 %collective-permute-start.4 = (bf16[6,2,6144]{2,1,0:T(2,128)(2,1)S(1)}, bf16[6,2,6144]{2,1,0:T(2,128)(2,1)S(1)}, u32[]{:S(2)}, u32[]{:S(2)}) collective-permute-start(bf16[6,2,6144]{2,1,0:T(2,128)(2,1)S(1)} %constant_dynamic-update-slice_fusion.6), channel_id=1, source_target_pairs={{0,32},{16,48},{32,64},{48,80},{64,96},{80,112},{96,128},{112,144}... | collective-permute-start | bytes 442376 | tf_op jit(solution)/shard_map/ppermute | solution.py:20
  70.4 7.9 %collective-permute-start.5 = (bf16[6,2,6144]{2,1,0:T(2,128)(2,1)S(1)}, bf16[6,2,6144]{2,1,0:T(2,128)(2,1)S(1)}, u32[]{:S(2)}, u32[]{:S(2)}) collective-permute-start(bf16[6,2,6144]{2,1,0:T(2,128)(2,1)S(1)} %constant_dynamic-update-slice_fusion.6), channel_id=1, source_target_pairs={{0,16},{16,32},{32,48},{48,64},{64,80},{80,96},{96,112},{112,128},... | collective-permute-start | bytes 442376 | tf_op jit(solution)/shard_map/ppermute | solution.py:20
  73.5 8.3 %collective-permute-start.6 = (bf16[6,2,6144]{2,1,0:T(2,128)(2,1)S(1)}, bf16[6,2,6144]{2,1,0:T(2,128)(2,1)S(1)}, u32[]{:S(2)}, u32[]{:S(2)}) collective-permute-start(bf16[6,2,6144]{2,1,0:T(2,128)(2,1)S(1)} %constant_dynamic-update-slice_fusion.6), channel_id=1, source_target_pairs={{16,0},{32,16},{48,32},{64,48},{80,64},{96,80},{112,96},{128,112},... | collective-permute-start | bytes 442376 | tf_op jit(solution)/shard_map/ppermute | solution.py:20
  74.8 14.2 %collective-permute-start.7 = (bf16[6,2,6144]{2,1,0:T(2,128)(2,1)S(1)}, bf16[6,2,6144]{2,1,0:T(2,128)(2,1)S(1)}, u32[]{:S(2)}, u32[]{:S(2)}) collective-permute-start(bf16[6,2,6144]{2,1,0:T(2,128)(2,1)S(1)} %constant_dynamic-update-slice_fusion.6), channel_id=1, source_target_pairs={{32,0},{48,16},{64,32},{80,48},{96,64},{112,80},{128,96},{144,112}... | collective-permute-start | bytes 442376 | tf_op jit(solution)/shard_map/ppermute | solution.py:20
  78.4 11.8 %copy-start.16 = (pred[12]{0:T(512)(128)(4,1)S(1)}, pred[12]{0:T(512)(128)(4,1)}, u32[]{:S(2)}) copy-start(pred[12]{0:T(512)(128)(4,1)} %copy-done.15) | copy-start | bytes 40
  78.4 11.8 %copy-start.18 = (pred[12]{0:T(512)(128)(4,1)S(1)}, pred[12]{0:T(512)(128)(4,1)}, u32[]{:S(2)}) copy-start(pred[12]{0:T(512)(128)(4,1)} %copy-done.17) | copy-start | bytes 40
  94.4 3.7 %copy-start.3 = (bf16[96,2,8,7,8]{0,4,3,2,1:T(8,128)(2,1)S(1)}, bf16[96,2,8,7,8]{0,4,3,2,1:T(8,128)(2,1)}, u32[]{:S(2)}) copy-start(bf16[96,2,8,7,8]{0,4,3,2,1:T(8,128)(2,1)} %get-tuple-element.186) | copy-start | bytes 516100
  94.5 3.7 %copy-start.2 = (bf16[96,2,8,7,8]{0,4,3,2,1:T(8,128)(2,1)S(1)}, bf16[96,2,8,7,8]{0,4,3,2,1:T(8,128)(2,1)}, u32[]{:S(2)}) copy-start(bf16[96,2,8,7,8]{0,4,3,2,1:T(8,128)(2,1)} %get-tuple-element.187) | copy-start | bytes 516100
  95.7 2.6 %copy-start.1 = (bf16[96,2,7,8,8]{0,4,3,2,1:T(8,128)(2,1)S(1)}, bf16[96,2,7,8,8]{0,4,3,2,1:T(8,128)(2,1)}, u32[]{:S(2)}) copy-start(bf16[96,2,7,8,8]{0,4,3,2,1:T(8,128)(2,1)} %get-tuple-element.188) | copy-start | bytes 516100
  96.7 1.7 copy-start.7
  103.4 30.8 %copy-start.8 = (bf16[144,96]{1,0:T(8,128)(2,1)S(1)}, bf16[144,96]{1,0:T(8,128)(2,1)}, u32[]{:S(2)}) copy-start(bf16[144,96]{1,0:T(8,128)(2,1)} %param.29) | copy-start | bytes 82948
  103.4 30.8 %copy-start.23 = (f32[96]{0:T(128)S(1)}, f32[96]{0:T(128)}, u32[]{:S(2)}) copy-start(f32[96]{0:T(128)} %param.28) | copy-start | bytes 1156
  104.4 22.9 %all-to-all-start.1 = ((bf16[96,16,128]{2,0,1:T(8,128)(2,1)}), bf16[96,16,128]{2,0,1:T(8,128)(2,1)S(1)}, u32[]{:S(2)}, u32[]{:S(2)}) async-start(bf16[96,16,128]{2,0,1:T(8,128)(2,1)} %copy.186), calls=%async_computation.1 | async-start | bytes 786432 | tf_op jit(solution)/shard_map/all_to_all | solution.py:144
  134.8 37.4 %copy-start.13 = (bf16[96,48]{0,1:T(8,128)(2,1)S(1)}, bf16[96,48]{0,1:T(8,128)(2,1)}, u32[]{:S(2)}) copy-start(bf16[96,48]{0,1:T(8,128)(2,1)} %param.30) | copy-start | bytes 27652
  178.9 17.7 %copy-start.12 = (s32[1024]{0:T(1024)S(1)}, s32[1024]{0:T(1024)}, u32[]{:S(2)}) copy-start(s32[1024]{0:T(1024)} %get-tuple-element.178) | copy-start | bytes 12292
  196.3 3.9 %copy-start.26 = (bf16[384,96]{0,1:T(8,128)(2,1)S(1)}, bf16[384,96]{0,1:T(8,128)(2,1)}, u32[]{:S(2)}) copy-start(bf16[384,96]{0,1:T(8,128)(2,1)} %param.32) | copy-start | bytes 221188
  196.3 3.9 %copy-start.27 = (f32[96]{0:T(128)S(1)}, f32[96]{0:T(128)}, u32[]{:S(2)}) copy-start(f32[96]{0:T(128)} %param.31) | copy-start | bytes 1156
  (6 other events, 5.6 us)
where the time goes:
time: 203 us; the launch traced here: 202 us
  local copies, waits for them, and re-layouts  70.3 us (35%)
  starting transfers between devices  43.8 us (22%)
  matrix products  23.1 us (11%)
  other arithmetic  19.3 us (10%)
  blocking collectives  17.2 us (8%)
  waiting for transfers between devices  15.4 us (8%)
  loops' own time  11.5 us (6%)
    ppermute x8, starting transfers between devices, from_behind(): return lax.ppermute(block, axis, route)  27 us
    all_to_all x1, blocking collectives, per_device(): lax.all_to_all(going_back, 'token', split_axis=1, concat_axis=1, tiled=True)  17.2 us
    another operation x1, loops' own time, per_device(): pieces = lax.map(attend_step, jnp.arange(total_steps, dtype=jnp.int32))  11.5 us
    dot_general x6, matrix products, attend_step(): jnp.einsum('hdq,hdk->hqk', query_part, key_part, precision=lax.Precision....  11 us
    ppermute x8, waiting for transfers between devices, from_behind(): return lax.ppermute(block, axis, route)  10.4 us
    another operation x4, local copies, waits for them, and re-layouts, cross_conv(): halo_flat.reshape(6, blocks_here, channels, EDGE, EDGE)  9.67 us
    all_to_all x1, starting transfers between devices, per_device(): lax.all_to_all(outgoing, 'token', split_axis=1, concat_axis=1, tiled=True)  8.42 us
    all_to_all x1, starting transfers between devices, per_device(): lax.all_to_all(labels, 'token', split_axis=1, concat_axis=1, tiled=True)  8.35 us
  transfers between devices with their start and end apart: 10, of which 3 were waited for; matrix products, arithmetic and copies ran while one was open for 30% of the time, Pallas kernels for 0%

commit v1 on v0

v1 whole, which is shorter than its diff:
```python
import functools
import math

import jax
import jax.numpy as jnp
from jax import lax
from jax.experimental import pallas as pl
from jax.experimental.pallas import tpu as pltpu
from jax.sharding import PartitionSpec as P

MESH = pl.DeviceIdType.MESH
F32 = jnp.float32
BF16 = jnp.bfloat16
I32 = jnp.int32

HEADS = 6
HD = 8
PATCH = 512
BLOCK = 512
FACE = 64
EPS = 1e-05
OFFS = (-2, -1, 1, 2)
SHIFTS = (64, -64, 8, -8, 1, -1)
AWAY = -1e30
NT_DIMS = (((1,), (1,)), ((), ()))
QROWS = 256
GROUP = 4


def dot(a, b):
    return jnp.dot(a, b, preferred_element_type=F32)


def dot_nt(a, b):
    return lax.dot_general(a, b, NT_DIMS, preferred_element_type=F32)


def face_index(face, place):
    high, low = place >> 3, place & 7
    if face == 0:
        return place
    if face == 1:
        return place + 448
    if face == 2:
        return high * 64 + low
    if face == 3:
        return high * 64 + low + 56
    if face == 4:
        return place * 8
    return place * 8 + 7


def store_one_hot(ref, row0, rows, lanes, index):
    width = index.shape[1]
    places = lax.broadcasted_iota(I32, (128, width), 0).astype(F32).astype(BF16)
    for part in range(rows // 128):
        here = jnp.where(index >> 7 == part, index & 127, -1).astype(F32).astype(BF16)
        hit = jnp.where(places == here, jnp.ones((), BF16), jnp.zeros((), BF16))
        ref[row0 + part * 128 : row0 + (part + 1) * 128, lanes] = hit


def column_of(row):
    size = row.shape[1]
    same = lax.broadcasted_iota(I32, (size, size), 0) == lax.broadcasted_iota(I32, (size, size), 1)
    return jnp.sum(jnp.where(same, row, 0.0), axis=1, keepdims=True)


def normalise(values, gain):
    center = values - jnp.mean(values, axis=0, keepdims=True)
    spread = jnp.mean(center * center, axis=0, keepdims=True)
    return center * lax.rsqrt(spread + EPS) * gain


def kernel(
    nb,
    nt,
    feats,
    occupancy,
    adjacency,
    serial_pos,
    conv_one,
    conv_two,
    gain_one,
    gain_two,
    gain_attn,
    w_qkv,
    w_out,
    gain_mlp,
    w_up,
    w_down,
    out_ref,
    signal,
    taps,
    conv_cat,
    send_pick,
    remote_pick,
    local_pick,
    spread_pick,
    halo_send,
    halo_recv,
    pack,
    label_send,
    label_recv,
    live_rows,
    place,
    block_out,
    data_send,
    data_recv,
    serial_acc,
    key_rows,
    query_rows,
    value_rows,
    self_rows,
    heads_out,
    back_send,
    back_recv,
    halo_sems,
    label_sems,
    data_sems,
    back_sems,
):
    channels, rows = feats.shape
    cap = pack.shape[0] // nt
    me_b = lax.axis_index("block")
    me_t = lax.axis_index("token")

    barrier = pltpu.get_barrier_semaphore()
    for off in OFFS:
        pl.semaphore_signal(
            barrier, inc=1, device_id={"block": lax.rem(me_b + off + nb, nb)}, device_id_type=MESH
        )
    for k in range(1, nt):
        pl.semaphore_signal(
            barrier, inc=1, device_id={"token": lax.rem(me_t + k, nt)}, device_id_type=MESH
        )

    def halo_copy(step, o):
        return pltpu.make_async_remote_copy(
            src_ref=halo_send.at[step, o],
            dst_ref=halo_recv.at[step, o],
            send_sem=halo_sems.at[0, step, o],
            recv_sem=halo_sems.at[1, step, o],
            device_id={"block": lax.rem(me_b + OFFS[o] + nb, nb)},
            device_id_type=MESH,
        )

    def token_copy(source, target, sems, k, step):
        return pltpu.make_async_remote_copy(
            src_ref=source.at[k],
            dst_ref=target.at[k],
            send_sem=sems.at[0, k],
            recv_sem=sems.at[1, k],
            device_id={"token": lax.rem(me_t + step + nt, nt)},
            device_id_type=MESH,
        )

    label_copy = lambda k: token_copy(label_send, label_recv, label_sems, k, k)
    data_copy = lambda k: token_copy(data_send, data_recv, data_sems, k, k)
    back_copy = lambda k: token_copy(back_send, back_recv, back_sems, k, -k)

    owner = {}
    index = {}
    for f in range(6):
        for b in range(2):
            owner[f, b] = adjacency[0, f, b]
            index[f, b] = adjacency[1, f, b]
    pairs = [(f, b) for f in range(6) for b in range(2)]
    lane = lax.broadcasted_iota(I32, (1, 128), 1)
    half, within = lane >> 6, lane & 63
    voxel_of = [face_index(f, within) for f in range(6)]
    for o, off in enumerate(OFFS):
        target = me_b + off
        count = jnp.int32(0)
        voxel = jnp.full((1, 128), -1, I32)
        for f, b in pairs:
            match = (owner[f, b] >= 0) & (owner[f, b] == target)
            slot = jnp.where(match, count, -1)
            count = count + jnp.where(match, 1, 0)
            voxel = jnp.where(half == slot, voxel_of[f] + b * BLOCK, voxel)
        store_one_hot(send_pick, 0, rows, slice(o * 128, (o + 1) * 128), voxel)

    occupied = occupancy[...] > 0
    field = jnp.where(occupied, feats[...].astype(F32), 0.0)
    signal[...] = field.astype(BF16)

    def send_halo(step):
        payload = dot(signal[...] if step == 0 else taps[0:channels, :], send_pick[...]).astype(BF16)
        for o in range(4):
            halo_send[step, o] = payload[:, o * 128 : (o + 1) * 128]

    send_halo(0)

    position = serial_pos[...]
    relative = ((position >> 10) - me_t + nt) & (nt - 1)
    sub16 = lax.broadcasted_iota(I32, (16, rows), 0)
    member = jnp.where(sub16 == relative, 1.0, 0.0)
    upto = lax.broadcasted_iota(I32, (128, 128), 0) <= lax.broadcasted_iota(I32, (128, 128), 1)
    upto = jnp.where(upto, 1.0, 0.0).astype(BF16)
    chunks = rows // 128
    stacked = jnp.concatenate(
        [member[:, c * 128 : (c + 1) * 128] for c in range(chunks)], axis=0
    ).astype(BF16)
    prefix = dot(stacked, upto)
    carry = jnp.zeros((16, 1), F32)
    ranks = []
    for c in range(chunks):
        piece = prefix[c * 16 : (c + 1) * 16, :]
        ranks.append(piece + carry - 1.0)
        carry = carry + piece[:, 127:128]
    slots = jnp.where(member > 0.5, jnp.concatenate(ranks, axis=1), -1.0).astype(I32)
    for k in range(nt):
        store_one_hot(pack, k * cap, cap, slice(0, rows), slots[k : k + 1, :])
    target_row = position & (rows - 1)
    facts = jnp.where(
        sub16 == 0,
        target_row >> 5,
        jnp.where(
            sub16 == 1,
            target_row & 31,
            jnp.where(sub16 == 2, jnp.where(occupied, 1, 0), jnp.where(sub16 == 3, 1, 0)),
        ),
    )
    facts = dot_nt(facts.astype(F32).astype(BF16), pack[...])
    goes_to = jnp.where(facts[3:4, :] > 0.5, facts[0:1, :] * 32.0 + facts[1:2, :], -1.0)
    sub8 = lax.broadcasted_iota(I32, (8, goes_to.shape[1]), 0)
    labels = jnp.where(sub8 == 0, goes_to, jnp.where(sub8 == 1, facts[2:3, :], 0.0))
    for k in range(nt):
        part = labels[:, k * cap : (k + 1) * cap]
        if k == 0:
            label_recv[0] = part
        else:
            label_send[k] = part

    pl.semaphore_wait(barrier, 4 + nt - 1)

    for o in range(4):
        halo_copy(0, o).start()
    for k in range(1, nt):
        label_copy(k).start()

    for a in range(3):
        for b in range(2):
            remote_src = jnp.full((1, 128), -1, I32)
            local_src = jnp.full((1, 128), -1, I32)
            for side in range(2):
                f = 2 * a + side
                own, idx = owner[f, b], index[f, b]
                key = (f ^ 1) * 2 + idx
                slot = jnp.int32(0)
                for f2, b2 in pairs:
                    if (f2, b2) != (f, b):
                        before = (owner[f2, b2] == own) & ((f2 ^ 1) * 2 + index[f2, b2] < key)
                        slot = slot + jnp.where(before, 1, 0)
                gap = me_b - own
                from_o = jnp.where(gap < 0, gap + 2, gap + 1)
                remote = (own >= 0) & (gap != 0)
                base = jnp.where(remote, from_o * 128 + slot * FACE, -4096)
                remote_src = jnp.where(half == side, within + base, remote_src)
                base = jnp.where((own >= 0) & (gap == 0), idx * BLOCK, -4096)
                local_src = jnp.where(half == side, voxel_of[f ^ 1] + base, local_src)
            lanes = slice((a * 2 + b) * 128, (a * 2 + b + 1) * 128)
            store_one_hot(remote_pick, 0, 512, lanes, remote_src)
            store_one_hot(local_pick, 0, rows, lanes, local_src)
    side_row = lax.broadcasted_iota(I32, (128, BLOCK), 0)
    voxel_lane = lax.broadcasted_iota(I32, (128, BLOCK), 1)
    for a in (1, 2):
        lower = face_index(2 * a, side_row & 63)
        upper = face_index(2 * a + 1, side_row & 63)
        hit = voxel_lane == jnp.where(side_row < 64, lower, upper)
        spread_pick[a - 1] = jnp.where(hit, 1.0, 0.0).astype(BF16)

    spot = lax.broadcasted_iota(I32, (1, rows), 1) & (BLOCK - 1)
    edges = [spot < 64, spot >= 448, (spot >> 3) & 7 == 0, (spot >> 3) & 7 == 7, spot & 7 == 0, spot & 7 == 7]
    on_edge = [jnp.where(e, 1.0, 0.0) for e in edges]

    def convolve(step, source, weight):
        for t in range(7):
            conv_cat[:, t * channels : (t + 1) * channels] = weight[t]
        for f in range(6):
            moved = pltpu.roll(source, SHIFTS[f] % rows, 1) * (1.0 - on_edge[f])
            taps[(f + 1) * channels : (f + 2) * channels, :] = moved.astype(BF16)
        halo = dot(taps[0:channels, :], local_pick[...])
        for o in range(4):
            halo_copy(step, o).wait_recv()
        received = jnp.concatenate([halo_recv[step, o] for o in range(4)], axis=1)
        halo = (halo + dot(received, remote_pick[...])).astype(BF16)
        for a in range(3):
            for b in range(2):
                lanes = slice((a * 2 + b) * 128, (a * 2 + b + 1) * 128)
                piece = halo[:, lanes]
                if a == 0:
                    gap = jnp.zeros((channels, BLOCK - 256), BF16)
                    wide = jnp.concatenate([piece, gap, piece], axis=1)
                else:
                    wide = dot(piece, spread_pick[a - 1]).astype(BF16)
                cols = slice(b * BLOCK, (b + 1) * BLOCK)
                for side in range(2):
                    f = 2 * a + side
                    tap_rows = slice((f + 1) * channels, (f + 2) * channels)
                    taps[tap_rows, cols] = taps[tap_rows, cols] + wide * on_edge[f][:, cols].astype(BF16)
        return dot(conv_cat[...], taps[...])

    taps[0:channels, :] = signal[...]
    summed = convolve(0, field, conv_one)
    middle = jnp.where(occupied, jnp.maximum(normalise(summed, column_of(gain_one[...])), 0.0), 0.0)
    middle = middle.astype(BF16)
    taps[0:channels, :] = middle
    send_halo(1)
    for o in range(4):
        halo_copy(1, o).start()

    for k in range(1, nt):
        label_copy(k).wait_recv()
    for k in range(nt):
        label = label_recv[k]
        lanes = slice(k * cap, (k + 1) * cap)
        store_one_hot(place, 0, rows, lanes, label[0:1, :].astype(I32))
        live_rows[:, lanes] = jnp.broadcast_to(label[1:2, :], (16, cap)).astype(BF16)
    query_rows[...] = jnp.zeros_like(query_rows)

    summed = convolve(1, middle.astype(F32), conv_two)
    result = jnp.maximum(signal[...].astype(F32) + normalise(summed, column_of(gain_two[...])), 0.0)
    result = jnp.where(occupied, result, 0.0).astype(BF16)
    block_out[...] = result
    normed = normalise(result.astype(F32), column_of(gain_attn[...])).astype(BF16)

    for g in range(nt // GROUP):
        span = slice(g * GROUP * cap, (g + 1) * GROUP * cap)
        packed = dot_nt(normed, pack[span, :]).astype(BF16)
        for j in range(GROUP):
            k = g * GROUP + j
            part = packed[:, j * cap : (j + 1) * cap]
            if k == 0:
                data_recv[0] = part
            else:
                data_send[k] = part
                data_copy(k).start()
    for g in range(nt // GROUP):
        span = slice(g * GROUP * cap, (g + 1) * GROUP * cap)
        for j in range(GROUP):
            if g + j:
                data_copy(g * GROUP + j).wait_recv()
        came = jnp.concatenate([data_recv[g * GROUP + j] for j in range(GROUP)], axis=1)
        came = jnp.concatenate([came, live_rows[:, span]], axis=0)
        part = dot_nt(came, place[:, span])
        serial_acc[...] = part if g == 0 else serial_acc[...] + part

    live = serial_acc[channels : channels + 1, :] > 0.5
    width = HEADS * HD
    projected = dot(w_qkv[...], serial_acc[0:channels, :].astype(BF16))
    scaled = projected[:width, :] * (math.log2(math.e) / math.sqrt(HD))
    query_high = scaled.astype(BF16).astype(F32)
    query_low = scaled - query_high
    keys = projected[width : 2 * width, :]
    key_high = keys.astype(BF16).astype(F32)
    key_low = keys - key_high
    values = projected[2 * width :, :]
    sub8 = lax.broadcasted_iota(I32, (8, rows), 0)
    ones8 = jnp.where(sub8 == 0, 1.0, 0.0)
    bias8 = jnp.where((sub8 == 0) & jnp.logical_not(live), AWAY, 0.0)
    key_parts = []
    patches = rows // PATCH
    for h in range(HEADS):
        own = slice(h * HD, (h + 1) * HD)
        key_parts += [key_high[own], key_low[own], key_high[own], bias8]
        query = jnp.concatenate([query_high[own], query_high[own], query_low[own], ones8], axis=0).astype(BF16)
        value_rows[h * 16 : (h + 1) * 16, :] = jnp.concatenate([values[own], ones8], axis=0).astype(BF16)
        for p in range(patches):
            query_rows[p * HEADS + h, h * 32 : (h + 1) * 32, :] = query[:, p * PATCH : (p + 1) * PATCH]
        alone = jnp.sum(scaled[own] * keys[own], axis=0, keepdims=True)
        self_rows[h] = jnp.where(live, AWAY, alone)
    key_parts.append(jnp.zeros((QROWS - HEADS * 32, rows), F32))
    key_rows[...] = jnp.concatenate(key_parts, axis=0).T.astype(BF16)

    def attend(p, h):
        cols = pl.ds(pl.multiple_of(p * PATCH, PATCH), PATCH)
        scores = dot(key_rows[cols, :], query_rows[p * HEADS + h])
        alone = self_rows[h, :, cols]
        largest = jnp.maximum(jnp.max(scores, axis=0, keepdims=True), alone)
        weights = jnp.exp2(scores - largest).astype(BF16)
        value = value_rows[pl.ds(pl.multiple_of(h * 16, 16), 16), cols]
        sums = dot(value, weights)
        own = jnp.exp2(alone - largest)
        top = sums[0:HD] + own * value[0:HD].astype(F32)
        heads_out[pl.ds(pl.multiple_of(h * HD, HD), HD), cols] = top / (sums[HD : HD + 1] + own)

    def attend_pair(i, _):
        p, h = i // (HEADS // 2), lax.rem(i, HEADS // 2) * 2
        attend(p, h)
        attend(p, h + 1)
        return 0

    lax.fori_loop(0, patches * HEADS // 2, attend_pair, 0)

    result = heads_out[...].astype(BF16)
    for g in range(nt // GROUP):
        back = dot(result, place[:, g * GROUP * cap : (g + 1) * GROUP * cap]).astype(BF16)
        for j in range(GROUP):
            k = g * GROUP + j
            part = back[:, j * cap : (j + 1) * cap]
            if k == 0:
                back_recv[0] = part
            else:
                back_send[k] = part
                back_copy(k).start()
    returned = None
    for g in range(nt // GROUP):
        for j in range(GROUP):
            if g + j:
                back_copy(g * GROUP + j).wait_recv()
        came = jnp.concatenate([back_recv[g * GROUP + j] for j in range(GROUP)], axis=1)
        part = dot(came, pack[g * GROUP * cap : (g + 1) * GROUP * cap, :])
        returned = part if g == 0 else returned + part
    attended = dot(w_out[...], returned.astype(BF16)).astype(BF16)
    gain = column_of(gain_mlp[...])
    for c in range(0, rows, 256):
        cols = slice(c, c + 256)
        combined = block_out[:, cols].astype(F32) + attended[:, cols].astype(F32)
        hidden = dot(w_up[...], normalise(combined, gain).astype(BF16))
        hidden = jax.nn.gelu(hidden).astype(BF16)
        summed = combined + dot(w_down[...], hidden)
        out_ref[:, cols] = jnp.where(occupied[:, cols], summed, 0.0).astype(BF16)

    for step in range(2):
        for o in range(4):
            halo_copy(step, o).wait_send()
    for k in range(1, nt):
        label_copy(k).wait_send()
        data_copy(k).wait_send()
        back_copy(k).wait_send()


def per_device(nb, nt, feats, occupancy, adjacency, serial_pos, conv_one, conv_two, gain_one, gain_two, gain_attn, w_qkv, w_out, gain_mlp, w_up, w_down):
    channels, rows = feats.shape
    slots = 2 * rows
    cap = slots // nt
    width = HEADS * HD
    vmem = pl.BlockSpec(memory_space=pltpu.VMEM)
    smem = pl.BlockSpec(memory_space=pltpu.SMEM)
    row = lambda x: x.reshape(1, -1)
    patches = rows // PATCH
    return pl.pallas_call(
        functools.partial(kernel, nb, nt),
        out_shape=jax.ShapeDtypeStruct((channels, rows), BF16),
        in_specs=[vmem, vmem, smem] + [vmem] * 11,
        out_specs=vmem,
        scratch_shapes=[
            pltpu.VMEM((channels, rows), BF16),
            pltpu.VMEM((7 * channels, rows), BF16),
            pltpu.VMEM((channels, 7 * channels), BF16),
            pltpu.VMEM((rows, 512), BF16),
            pltpu.VMEM((512, 768), BF16),
            pltpu.VMEM((rows, 768), BF16),
            pltpu.VMEM((2, 128, BLOCK), BF16),
            pltpu.VMEM((2, 4, channels, 128), BF16),
            pltpu.VMEM((2, 4, channels, 128), BF16),
            pltpu.VMEM((slots, rows), BF16),
            pltpu.VMEM((nt, 8, cap), F32),
            pltpu.VMEM((nt, 8, cap), F32),
            pltpu.VMEM((16, slots), BF16),
            pltpu.VMEM((rows, slots), BF16),
            pltpu.VMEM((channels, rows), BF16),
            pltpu.VMEM((nt, channels, cap), BF16),
            pltpu.VMEM((nt, channels, cap), BF16),
            pltpu.VMEM((channels + 16, rows), F32),
            pltpu.VMEM((rows, QROWS), BF16),
            pltpu.VMEM((patches * HEADS, QROWS, PATCH), BF16),
            pltpu.VMEM((HEADS * 16, rows), BF16),
            pltpu.VMEM((HEADS, 1, rows), F32),
            pltpu.VMEM((width, rows), F32),
            pltpu.VMEM((nt, width, cap), BF16),
            pltpu.VMEM((nt, width, cap), BF16),
            pltpu.SemaphoreType.DMA((2, 2, 4)),
            pltpu.SemaphoreType.DMA((2, nt)),
            pltpu.SemaphoreType.DMA((2, nt)),
            pltpu.SemaphoreType.DMA((2, nt)),
        ],
        compiler_params=pltpu.CompilerParams(collective_id=0, has_side_effects=True),
        name="voxel_step",
    )(
        feats,
        row(occupancy),
        adjacency,
        row(serial_pos),
        conv_one,
        conv_two,
        row(gain_one),
        row(gain_two),
        row(gain_attn),
        w_qkv,
        w_out,
        row(gain_mlp),
        w_up,
        w_down,
    )


def solution(mesh):
    nb, nt = mesh.shape["block"], mesh.shape["token"]
    split = ("block", "token")
    in_specs = (P(None, split), P(split), P(None, None, split), P(split)) + (P(),) * 10
    return jax.shard_map(
        functools.partial(per_device, nb, nt),
        mesh=mesh,
        in_specs=in_specs,
        out_specs=P(None, split),
        check_vma=False,
    )
```

time: 203 us -> 62.7 us (0.31)
  local copies, waits for them, and re-layouts: 70.3 us -> 5.32 us
  Pallas kernels: 0 us -> 57.1 us
  starting transfers between devices: 43.8 us -> 0 us
  matrix products: 23.1 us -> 0 us
  other arithmetic: 19.3 us -> 0 us
  blocking collectives: 17.2 us -> 0 us
  waiting for transfers between devices: 15.4 us -> 0 us
  loops' own time: 11.5 us -> 0 us
    pallas_call x0 -> x1, Pallas kernels: none -> 57.1 us  [per_device(): pl.pallas_call(functools.partial(kernel, nb, nt), out_shape=jax.ShapeDtyp...]
    ppermute x8 -> x0, starting transfers between devices: 27 us -> none  [from_behind(): return lax.ppermute(block, axis, route)]
    scatter x5 -> x0, local copies, waits for them, and re-layouts: 26.3 us -> none  [the longest x1 8.04 us: per_device(): jnp.zeros((rows_here,), jnp.int32).at[in_labels[0]]]
    dot_general x29 -> x0, matrix products: 23.1 us -> none  [the longest x6 11 us: attend_step(): jnp.einsum('hdq,hdk->hqk', query_part, key_part, precision=lax.Precision....]
    all_to_all x1 -> x0, blocking collectives: 17.2 us -> none  [per_device(): lax.all_to_all(going_back, 'token', split_axis=1, concat_axis=1, tiled=True)]
    all_to_all x2 -> x0, starting transfers between devices: 16.8 us -> none  [the longest x1 8.42 us: per_device(): lax.all_to_all(outgoing, 'token', split_axis=1, concat_axis=1, tiled=True)]
    another operation x28 -> x0, local copies, waits for them, and re-layouts: 15.6 us -> none  [the longest x4 9.67 us: cross_conv(): halo_flat.reshape(6, blocks_here, channels, EDGE, EDGE)]
    another operation x1 -> x0, loops' own time: 11.5 us -> none  [per_device(): pieces = lax.map(attend_step, jnp.arange(total_steps, dtype=jnp.int32))]
  transfers between devices with their start and end apart: 10 -> 0, of which waited for: 3 -> 0; matrix products, arithmetic and copies ran while one was open for 30% -> 0% of each run, Pallas kernels for 0% -> 0%
where the time goes in v1:
time: 62.7 us; the launch traced here: 62.4 us
  Pallas kernels  57.1 us (91%)
  local copies, waits for them, and re-layouts  5.32 us (8%)
    pallas_call x1, Pallas kernels, per_device(): pl.pallas_call(functools.partial(kernel, nb, nt), out_shape=jax.ShapeDtyp...  57.1 us
    unnamed x6, local copies, waits for them, and re-layouts  5.32 us

profile of v1, /device:TPU:1, one launch (start us, length us, event | category | flops | bytes accessed | tf_op | source)
XLA Modules:
  0.0 62.4 jit_solution(8766537951461097292)
XLA Ops:
  0.0 0.0 copy-start
  0.0 1.4 %copy.15.adjacency = s32[2,6,2]{2,1,0:T(8,128)} copy(s32[2,6,2]{1,2,0:T(2,128)} %param.16) | data formatting | bytes 192 | tf_op args[2]
  1.4 0.0 copy-done
  1.4 0.7 %copy.16.w_out = bf16[96,48]{1,0:T(8,128)(2,1)} copy(bf16[96,48]{0,1:T(8,128)(2,1)S(1)} %copy-done) | data formatting | bytes 18432 | tf_op args[10]
  2.1 1.6 %copy.17.w_up = bf16[384,96]{1,0:T(8,128)(2,1)} copy(bf16[384,96]{0,1:T(8,128)(2,1)} %param.26) | data formatting | bytes 147456 | tf_op args[12]
  3.7 57.1 %voxel_step.1 = bf16[96,1024]{1,0:T(8,128)(2,1)} custom-call(bf16[96,1024]{1,0:T(8,128)(2,1)} %feats.1, s32[1,1024]{1,0:T(1,128)} %bitcast.6, s32[2,6,2]{2,1,0:T(8,128)} %copy.15.adjacency, s32[1,1024]{1,0:T(1,128)} %bitcast.7, bf16[7,96,96]{2,1,0:T(8,128)(2,1)} %conv_one.1, bf16[7,96,96]{2,1,0:T(8,128)(2,1)} %conv_two.1, f32[1,96]{1,0:T(1,128)} %bitcast.8, ...), custom_call_target="tpu_custom_call" | custom-call | tf_op jit(solution)/shard_map/voxel_step/pallas_call | solution.py:442
  60.8 1.6 %copy.19 = bf16[96,1024]{1,0:T(8,128)(2,1)} copy(bf16[96,1024]{1,0:T(8,128)(2,1)} %voxel_step.1) | data formatting | bytes 393216
Async XLA Ops:
  0.0 1.4 %copy-start = (bf16[96,48]{0,1:T(8,128)(2,1)S(1)}, bf16[96,48]{0,1:T(8,128)(2,1)}, u32[]{:S(2)}) copy-start(bf16[96,48]{0,1:T(8,128)(2,1)} %param.24) | copy-start | bytes 27652

commit v2 on v1

v2 whole, which is shorter than its diff:
```python
import functools
import math

import jax
import jax.numpy as jnp
from jax import lax
from jax.experimental import pallas as pl
from jax.experimental.pallas import tpu as pltpu
from jax.sharding import PartitionSpec as P

MESH = pl.DeviceIdType.MESH
F32 = jnp.float32
BF16 = jnp.bfloat16
I32 = jnp.int32

HEADS = 6
HD = 8
PATCH = 512
BLOCK = 512
FACE = 64
EPS = 1e-05
OFFS = (-2, -1, 1, 2)
SHIFTS = (64, -64, 8, -8, 1, -1)
AWAY = -1e30
NT_DIMS = (((1,), (1,)), ((), ()))
QROWS = 256
GROUP = 4
INPUTS = 14
RUNS = ((0, 3), (4, 5))
HEAD_ROWS = (slice(0, 32), slice(32, 48))
VMEM_LIMIT = 36 * 1024 * 1024


def dot(a, b):
    return jnp.dot(a, b, preferred_element_type=F32)


def dot_nt(a, b):
    return lax.dot_general(a, b, NT_DIMS, preferred_element_type=F32)


def face_index(face, place):
    high, low = place >> 3, place & 7
    if face == 0:
        return place
    if face == 1:
        return place + 448
    if face == 2:
        return high * 64 + low
    if face == 3:
        return high * 64 + low + 56
    if face == 4:
        return place * 8
    return place * 8 + 7


def store_one_hot(ref, row0, rows, lanes, index):
    width = index.shape[1]
    places = lax.broadcasted_iota(I32, (128, width), 0).astype(F32).astype(BF16)
    for part in range(rows // 128):
        here = jnp.where(index >> 7 == part, index & 127, -1).astype(F32).astype(BF16)
        hit = jnp.where(places == here, jnp.ones((), BF16), jnp.zeros((), BF16))
        ref[row0 + part * 128 : row0 + (part + 1) * 128, lanes] = hit


def column_of(row):
    size = row.shape[1]
    same = lax.broadcasted_iota(I32, (size, size), 0) == lax.broadcasted_iota(I32, (size, size), 1)
    return jnp.sum(jnp.where(same, row, 0.0), axis=1, keepdims=True)


def normalise(values, gain):
    center = values - jnp.mean(values, axis=0, keepdims=True)
    spread = jnp.mean(center * center, axis=0, keepdims=True)
    return center * lax.rsqrt(spread + EPS) * gain


def kernel(
    nb,
    nt,
    *refs,
):
    sources, out_ref, held = refs[:INPUTS], refs[INPUTS], refs[INPUTS + 1 : 2 * INPUTS + 1]
    (
        signal,
        taps,
        conv_cat,
        send_pick,
        remote_pick,
        local_pick,
        spread_pick,
        halo_send,
        halo_recv,
        pack,
        label_send,
        label_recv,
        live_rows,
        place,
        block_out,
        data_send,
        data_recv,
        serial_acc,
        key_rows,
        query_rows,
        value_rows,
        self_rows,
        heads_out,
        back_send,
        back_recv,
        halo_sems,
        label_sems,
        data_sems,
        back_sems,
        input_sems,
    ) = refs[2 * INPUTS + 1 :]
    loads = [pltpu.make_async_copy(sources[i], held[i], input_sems.at[i]) for i in range(INPUTS)]
    for load in loads:
        load.start()
    (
        feats,
        occupancy,
        adjacency,
        serial_pos,
        conv_one,
        conv_two,
        gain_one,
        gain_two,
        gain_attn,
        w_qkv,
        w_out,
        gain_mlp,
        w_up,
        w_down,
    ) = held
    channels, rows = feats.shape
    cap = pack.shape[0] // nt
    me_b = lax.axis_index("block")
    order = sorted(range(nt), key=lambda k: (-min(k, nt - k), k))
    me_t = lax.axis_index("token")

    barrier = pltpu.get_barrier_semaphore()
    for off in OFFS:
        pl.semaphore_signal(
            barrier, inc=1, device_id={"block": lax.rem(me_b + off + nb, nb)}, device_id_type=MESH
        )
    for k in range(1, nt):
        pl.semaphore_signal(
            barrier, inc=1, device_id={"token": lax.rem(me_t + k, nt)}, device_id_type=MESH
        )

    def halo_copy(step, o):
        return pltpu.make_async_remote_copy(
            src_ref=halo_send.at[step, o],
            dst_ref=halo_recv.at[step, o],
            send_sem=halo_sems.at[0, step, o],
            recv_sem=halo_sems.at[1, step, o],
            device_id={"block": lax.rem(me_b + OFFS[o] + nb, nb)},
            device_id_type=MESH,
        )

    def token_copy(source, target, sems, k, step):
        return pltpu.make_async_remote_copy(
            src_ref=source.at[k],
            dst_ref=target.at[k],
            send_sem=sems.at[0, k],
            recv_sem=sems.at[1, k],
            device_id={"token": lax.rem(me_t + step + nt, nt)},
            device_id_type=MESH,
        )

    label_copy = lambda k: token_copy(label_send, label_recv, label_sems, k, k)
    data_copy = lambda k: token_copy(data_send, data_recv, data_sems, k, k)

    def back_copy(t, k):
        return pltpu.make_async_remote_copy(
            src_ref=back_send.at[k, HEAD_ROWS[t]],
            dst_ref=back_recv.at[k, HEAD_ROWS[t]],
            send_sem=back_sems.at[0, t, k],
            recv_sem=back_sems.at[1, t, k],
            device_id={"token": lax.rem(me_t - k + nt, nt)},
            device_id_type=MESH,
        )


    for i in range(4):
        loads[i].wait()
    owner = {}
    index = {}
    for f in range(6):
        for b in range(2):
            owner[f, b] = adjacency[0, b, f]
            index[f, b] = adjacency[1, b, f]
    pairs = [(f, b) for f in range(6) for b in range(2)]
    lane = lax.broadcasted_iota(I32, (1, 128), 1)
    half, within = lane >> 6, lane & 63
    voxel_of = [face_index(f, within) for f in range(6)]
    for o, off in enumerate(OFFS):
        target = me_b + off
        count = jnp.int32(0)
        voxel = jnp.full((1, 128), -1, I32)
        for f, b in pairs:
            match = (owner[f, b] >= 0) & (owner[f, b] == target)
            slot = jnp.where(match, count, -1)
            count = count + jnp.where(match, 1, 0)
            voxel = jnp.where(half == slot, voxel_of[f] + b * BLOCK, voxel)
        store_one_hot(send_pick, 0, rows, slice(o * 128, (o + 1) * 128), voxel)

    occupied = occupancy[...] > 0
    field = jnp.where(occupied, feats[...].astype(F32), 0.0)
    signal[...] = field.astype(BF16)

    def send_halo(step):
        payload = dot(signal[...] if step == 0 else taps[0:channels, :], send_pick[...]).astype(BF16)
        for o in range(4):
            halo_send[step, o] = payload[:, o * 128 : (o + 1) * 128]

    send_halo(0)

    pl.semaphore_wait(barrier, 4 + nt - 1)

    for o in range(4):
        halo_copy(0, o).start()

    for a in range(3):
        for b in range(2):
            remote_src = jnp.full((1, 128), -1, I32)
            local_src = jnp.full((1, 128), -1, I32)
            for side in range(2):
                f = 2 * a + side
                own, idx = owner[f, b], index[f, b]
                key = (f ^ 1) * 2 + idx
                slot = jnp.int32(0)
                for f2, b2 in pairs:
                    if (f2, b2) != (f, b):
                        before = (owner[f2, b2] == own) & ((f2 ^ 1) * 2 + index[f2, b2] < key)
                        slot = slot + jnp.where(before, 1, 0)
                gap = me_b - own
                from_o = jnp.where(gap < 0, gap + 2, gap + 1)
                remote = (own >= 0) & (gap != 0)
                base = jnp.where(remote, from_o * 128 + slot * FACE, -4096)
                remote_src = jnp.where(half == side, within + base, remote_src)
                base = jnp.where((own >= 0) & (gap == 0), idx * BLOCK, -4096)
                local_src = jnp.where(half == side, voxel_of[f ^ 1] + base, local_src)
            lanes = slice((a * 2 + b) * 128, (a * 2 + b + 1) * 128)
            store_one_hot(remote_pick, 0, 512, lanes, remote_src)
            store_one_hot(local_pick, 0, rows, lanes, local_src)
    side_row = lax.broadcasted_iota(I32, (128, BLOCK), 0)
    voxel_lane = lax.broadcasted_iota(I32, (128, BLOCK), 1)
    for a in (1, 2):
        lower = face_index(2 * a, side_row & 63)
        upper = face_index(2 * a + 1, side_row & 63)
        hit = voxel_lane == jnp.where(side_row < 64, lower, upper)
        spread_pick[a - 1] = jnp.where(hit, 1.0, 0.0).astype(BF16)

    spot = lax.broadcasted_iota(I32, (1, rows), 1) & (BLOCK - 1)
    edges = [spot < 64, spot >= 448, (spot >> 3) & 7 == 0, (spot >> 3) & 7 == 7, spot & 7 == 0, spot & 7 == 7]
    on_edge = [jnp.where(e, 1.0, 0.0) for e in edges]

    def convolve(step, source, weight):
        for t in range(7):
            conv_cat[:, t * channels : (t + 1) * channels] = weight[t]
        for f in range(6):
            moved = pltpu.roll(source, SHIFTS[f] % rows, 1) * (1.0 - on_edge[f])
            taps[(f + 1) * channels : (f + 2) * channels, :] = moved.astype(BF16)
        halo = dot(taps[0:channels, :], local_pick[...])
        for o in range(4):
            halo_copy(step, o).wait_recv()
        received = jnp.concatenate([halo_recv[step, o] for o in range(4)], axis=1)
        halo = (halo + dot(received, remote_pick[...])).astype(BF16)
        for a in range(3):
            for b in range(2):
                lanes = slice((a * 2 + b) * 128, (a * 2 + b + 1) * 128)
                piece = halo[:, lanes]
                if a == 0:
                    gap = jnp.zeros((channels, BLOCK - 256), BF16)
                    wide = jnp.concatenate([piece, gap, piece], axis=1)
                else:
                    wide = dot(piece, spread_pick[a - 1]).astype(BF16)
                cols = slice(b * BLOCK, (b + 1) * BLOCK)
                for side in range(2):
                    f = 2 * a + side
                    tap_rows = slice((f + 1) * channels, (f + 2) * channels)
                    taps[tap_rows, cols] = taps[tap_rows, cols] + wide * on_edge[f][:, cols].astype(BF16)
        return dot(conv_cat[...], taps[...])

    for i in range(4, INPUTS):
        loads[i].wait()
    taps[0:channels, :] = signal[...]
    summed = convolve(0, field, conv_one)
    middle = jnp.where(occupied, jnp.maximum(normalise(summed, column_of(gain_one[...])), 0.0), 0.0)
    middle = middle.astype(BF16)
    taps[0:channels, :] = middle
    send_halo(1)
    for o in range(4):
        halo_copy(1, o).start()

    position = serial_pos[...]
    relative = ((position >> 10) - me_t + nt) & (nt - 1)
    sub16 = lax.broadcasted_iota(I32, (16, rows), 0)
    member = jnp.where(sub16 == relative, 1.0, 0.0)
    upto = lax.broadcasted_iota(I32, (128, 128), 0) <= lax.broadcasted_iota(I32, (128, 128), 1)
    upto = jnp.where(upto, 1.0, 0.0).astype(BF16)
    chunks = rows // 128
    stacked = jnp.concatenate(
        [member[:, c * 128 : (c + 1) * 128] for c in range(chunks)], axis=0
    ).astype(BF16)
    prefix = dot(stacked, upto)
    carry = jnp.zeros((16, 1), F32)
    ranks = []
    for c in range(chunks):
        piece = prefix[c * 16 : (c + 1) * 16, :]
        ranks.append(piece + carry - 1.0)
        carry = carry + piece[:, 127:128]
    slots = jnp.where(member > 0.5, jnp.concatenate(ranks, axis=1), -1.0).astype(I32)
    for k in range(nt):
        store_one_hot(pack, k * cap, cap, slice(0, rows), slots[k : k + 1, :])
    target_row = position & (rows - 1)
    facts = jnp.where(
        sub16 == 0,
        target_row >> 5,
        jnp.where(
            sub16 == 1,
            target_row & 31,
            jnp.where(sub16 == 2, jnp.where(occupied, 1, 0), jnp.where(sub16 == 3, 1, 0)),
        ),
    )
    facts = dot_nt(facts.astype(F32).astype(BF16), pack[...])
    goes_to = jnp.where(facts[3:4, :] > 0.5, facts[0:1, :] * 32.0 + facts[1:2, :], -1.0)
    sub8 = lax.broadcasted_iota(I32, (8, goes_to.shape[1]), 0)
    labels = jnp.where(sub8 == 0, goes_to, jnp.where(sub8 == 1, facts[2:3, :], 0.0))
    for k in range(nt):
        part = labels[:, k * cap : (k + 1) * cap]
        if k == 0:
            label_recv[0] = part
        else:
            label_send[k] = part

    for k in range(1, nt):
        label_copy(k).start()

    summed = convolve(1, middle.astype(F32), conv_two)
    result = jnp.maximum(signal[...].astype(F32) + normalise(summed, column_of(gain_two[...])), 0.0)
    result = jnp.where(occupied, result, 0.0).astype(BF16)
    block_out[...] = result
    normed = normalise(result.astype(F32), column_of(gain_attn[...])).astype(BF16)

    for g in range(nt // GROUP):
        ks = order[g * GROUP : (g + 1) * GROUP]
        chosen = jnp.concatenate([pack[k * cap : (k + 1) * cap, :] for k in ks], axis=0)
        packed = dot_nt(normed, chosen).astype(BF16)
        for j, k in enumerate(order[g * GROUP : (g + 1) * GROUP]):
            part = packed[:, j * cap : (j + 1) * cap]
            if k == 0:
                data_recv[0] = part
            else:
                data_send[k] = part
                data_copy(k).start()

    for k in range(1, nt):
        label_copy(k).wait_recv()
    for k in range(nt):
        label = label_recv[k]
        lanes = slice(k * cap, (k + 1) * cap)
        store_one_hot(place, 0, rows, lanes, label[0:1, :].astype(I32))
        live_rows[:, lanes] = jnp.broadcast_to(label[1:2, :], (16, cap)).astype(BF16)
    query_rows[...] = jnp.zeros_like(query_rows)
    w_out_here = w_out[...].astype(F32).T.astype(BF16)
    w_up_here = w_up[...].astype(F32).T.astype(BF16)
    for g in range(nt // GROUP):
        ks = order[g * GROUP : (g + 1) * GROUP]
        for k in ks:
            if k:
                data_copy(k).wait_recv()
        came = jnp.concatenate(
            [
                jnp.concatenate([data_recv[k], live_rows[:, k * cap : (k + 1) * cap]], axis=0)
                for k in ks
            ],
            axis=1,
        )
        chosen = jnp.concatenate([place[:, k * cap : (k + 1) * cap] for k in ks], axis=1)
        part = dot_nt(came, chosen)
        serial_acc[...] = part if g == 0 else serial_acc[...] + part

    live = serial_acc[channels : channels + 1, :] > 0.5
    width = HEADS * HD
    projected = dot(w_qkv[...], serial_acc[0:channels, :].astype(BF16))
    scaled = projected[:width, :] * (math.log2(math.e) / math.sqrt(HD))
    query_high = scaled.astype(BF16).astype(F32)
    query_low = scaled - query_high
    keys = projected[width : 2 * width, :]
    key_high = keys.astype(BF16).astype(F32)
    key_low = keys - key_high
    values = projected[2 * width :, :]
    sub8 = lax.broadcasted_iota(I32, (8, rows), 0)
    ones8 = jnp.where(sub8 == 0, 1.0, 0.0)
    bias8 = jnp.where((sub8 == 0) & jnp.logical_not(live), AWAY, 0.0)
    key_parts = []
    patches = rows // PATCH
    for h in range(HEADS):
        own = slice(h * HD, (h + 1) * HD)
        key_parts += [key_high[own], key_low[own], key_high[own], bias8]
        query = jnp.concatenate([query_high[own], query_high[own], query_low[own], ones8], axis=0).astype(BF16)
        value_rows[h * 16 : (h + 1) * 16, :] = jnp.concatenate([values[own], ones8], axis=0).astype(BF16)
        for p in range(patches):
            query_rows[p * HEADS + h, h * 32 : (h + 1) * 32, :] = query[:, p * PATCH : (p + 1) * PATCH]
        alone = jnp.sum(scaled[own] * keys[own], axis=0, keepdims=True)
        self_rows[h] = jnp.where(live, AWAY, alone)
    key_parts.append(jnp.zeros((QROWS - HEADS * 32, rows), F32))
    key_rows[...] = jnp.concatenate(key_parts, axis=0).T.astype(BF16)

    def score(p, h):
        return dot(key_rows[p * PATCH : (p + 1) * PATCH, :], query_rows[p * HEADS + h])

    def attend(p, h, scores):
        cols = slice(p * PATCH, (p + 1) * PATCH)
        alone = self_rows[h, :, cols]
        largest = jnp.maximum(jnp.max(scores, axis=0, keepdims=True), alone)
        weights = jnp.exp2(scores - largest).astype(BF16)
        value = value_rows[h * 16 : (h + 1) * 16, cols]
        sums = dot(value, weights)
        own = jnp.exp2(alone - largest)
        top = sums[0:HD] + own * value[0:HD].astype(F32)
        heads_out[h * HD : (h + 1) * HD, cols] = top / (sums[HD : HD + 1] + own)

    def to_slots(heads, p):
        part = heads_out[heads[0] * HD : (heads[1] + 1) * HD, p * PATCH : (p + 1) * PATCH].astype(BF16)
        return dot(part, place[p * PATCH : (p + 1) * PATCH, :])

    def give_back(t, slots):
        slots = slots.astype(BF16)
        for k in order:
            part = slots[:, k * cap : (k + 1) * cap]
            if k == 0:
                back_recv[0, HEAD_ROWS[t]] = part
            else:
                back_send[k, HEAD_ROWS[t]] = part
        for k in order:
            if k:
                back_copy(t, k).start()

    waves = [(t, p) for t in range(len(RUNS)) for p in range(patches)]
    units = [(t, p, h) for t, p in waves for h in range(RUNS[t][0], RUNS[t][1] + 1)]
    ahead = score(*units[0][1:])
    slots = None
    for i, (t, p, h) in enumerate(units):
        scores = ahead
        if i + 1 < len(units):
            ahead = score(*units[i + 1][1:])
        attend(p, h, scores)
        if h == RUNS[t][1]:
            part = to_slots(RUNS[t], p)
            slots = part if p == 0 else slots + part
            if p == patches - 1:
                give_back(t, slots)

    returned = None
    for g in range(nt // GROUP):
        ks = order[g * GROUP : (g + 1) * GROUP]
        for k in ks:
            if k:
                for t in range(len(RUNS)):
                    back_copy(t, k).wait_recv()
        came = jnp.concatenate([back_recv[k] for k in ks], axis=1)
        part = dot(came, jnp.concatenate([pack[k * cap : (k + 1) * cap, :] for k in ks], axis=0))
        returned = part if g == 0 else returned + part
    attended = dot(w_out_here, returned.astype(BF16)).astype(BF16)
    gain = column_of(gain_mlp[...])
    for c in range(0, rows, 256):
        cols = slice(c, c + 256)
        combined = block_out[:, cols].astype(F32) + attended[:, cols].astype(F32)
        hidden = dot(w_up_here, normalise(combined, gain).astype(BF16))
        hidden = jax.nn.gelu(hidden).astype(BF16)
        summed = combined + dot(w_down[...], hidden)
        out_ref[:, cols] = jnp.where(occupied[:, cols], summed, 0.0).astype(BF16)

    for step in range(2):
        for o in range(4):
            halo_copy(step, o).wait_send()
    for k in range(1, nt):
        label_copy(k).wait_send()
        data_copy(k).wait_send()
        for t in range(len(RUNS)):
            back_copy(t, k).wait_send()


def per_device(nb, nt, feats, occupancy, adjacency, serial_pos, conv_one, conv_two, gain_one, gain_two, gain_attn, w_qkv, w_out, gain_mlp, w_up, w_down):
    channels, rows = feats.shape
    slots = 2 * rows
    cap = slots // nt
    width = HEADS * HD
    row = lambda x: x.reshape(1, -1)
    patches = rows // PATCH
    inputs = (
        feats,
        row(occupancy),
        adjacency.transpose(0, 2, 1),
        row(serial_pos),
        conv_one,
        conv_two,
        row(gain_one),
        row(gain_two),
        row(gain_attn),
        w_qkv,
        w_out.T,
        row(gain_mlp),
        w_up.T,
        w_down,
    )
    return pl.pallas_call(
        functools.partial(kernel, nb, nt),
        out_shape=jax.ShapeDtypeStruct((channels, rows), BF16),
        in_specs=[pl.BlockSpec(memory_space=pltpu.HBM)] * INPUTS,
        out_specs=pl.BlockSpec(memory_space=pltpu.VMEM),
        scratch_shapes=[
            pltpu.SMEM(x.shape, x.dtype) if i == 2 else pltpu.VMEM(x.shape, x.dtype)
            for i, x in enumerate(inputs)
        ]
        + [
            pltpu.VMEM((channels, rows), BF16),
            pltpu.VMEM((7 * channels, rows), BF16),
            pltpu.VMEM((channels, 7 * channels), BF16),
            pltpu.VMEM((rows, 512), BF16),
            pltpu.VMEM((512, 768), BF16),
            pltpu.VMEM((rows, 768), BF16),
            pltpu.VMEM((2, 128, BLOCK), BF16),
            pltpu.VMEM((2, 4, channels, 128), BF16),
            pltpu.VMEM((2, 4, channels, 128), BF16),
            pltpu.VMEM((slots, rows), BF16),
            pltpu.VMEM((nt, 8, cap), F32),
            pltpu.VMEM((nt, 8, cap), F32),
            pltpu.VMEM((16, slots), BF16),
            pltpu.VMEM((rows, slots), BF16),
            pltpu.VMEM((channels, rows), BF16),
            pltpu.VMEM((nt, channels, cap), BF16),
            pltpu.VMEM((nt, channels, cap), BF16),
            pltpu.VMEM((channels + 16, rows), F32),
            pltpu.VMEM((rows, QROWS), BF16),
            pltpu.VMEM((patches * HEADS, QROWS, PATCH), BF16),
            pltpu.VMEM((HEADS * 16, rows), BF16),
            pltpu.VMEM((HEADS, 1, rows), F32),
            pltpu.VMEM((width, rows), F32),
            pltpu.VMEM((nt, width, cap), BF16),
            pltpu.VMEM((nt, width, cap), BF16),
            pltpu.SemaphoreType.DMA((2, 2, 4)),
            pltpu.SemaphoreType.DMA((2, nt)),
            pltpu.SemaphoreType.DMA((2, nt)),
            pltpu.SemaphoreType.DMA((2, len(RUNS), nt)),
            pltpu.SemaphoreType.DMA((INPUTS,)),
        ],
        compiler_params=pltpu.CompilerParams(
            collective_id=0, has_side_effects=True, vmem_limit_bytes=VMEM_LIMIT
        ),
        name="voxel_step",
    )(*[pltpu.with_memory_space_constraint(x, pltpu.HBM) for x in inputs])


def solution(mesh):
    nb, nt = mesh.shape["block"], mesh.shape["token"]
    split = ("block", "token")
    in_specs = (P(None, split), P(split), P(None, None, split), P(split)) + (P(),) * 10
    return jax.shard_map(
        functools.partial(per_device, nb, nt),
        mesh=mesh,
        in_specs=in_specs,
        out_specs=P(None, split),
        check_vma=False,
    )
```

time: 62.7 us -> 52.7 us (0.84)
  Pallas kernels: 57.1 us -> 51.9 us
  local copies, waits for them, and re-layouts: 5.32 us -> 0.68 us
    pallas_call x1, Pallas kernels: 57.1 us -> 51.9 us  [per_device(): pl.pallas_call(functools.partial(kernel, nb, nt), out_shape=jax.ShapeDtyp...]
    unnamed x6 -> x1, local copies, waits for them, and re-layouts: 5.32 us -> 0.68 us
where the time goes in v2:
time: 52.7 us; the launch traced here: 52.6 us
  Pallas kernels  51.9 us (98%)
  local copies, waits for them, and re-layouts  0.68 us (1%)
    pallas_call x1, Pallas kernels, per_device(): pl.pallas_call(functools.partial(kernel, nb, nt), out_shape=jax.ShapeDtyp...  51.9 us

profile of v2, /device:TPU:1, one launch (start us, length us, event | category | flops | bytes accessed | tf_op | source)
XLA Modules:
  0.0 52.6 jit_solution(3366354657767755767)
XLA Ops:
  0.0 51.9 %voxel_step.1 = bf16[96,1024]{1,0:T(8,128)(2,1)S(1)} custom-call(bf16[96,1024]{1,0:T(8,128)(2,1)} %refs_0_.1, s32[1,1024]{1,0:T(1,128)} %bitcast.11, s32[2,2,6]{2,1,0:T(2,128)} %bitcast.13, s32[1,1024]{1,0:T(1,128)} %bitcast.12, bf16[7,96,96]{2,1,0:T(8,128)(2,1)} %refs_4_.1, bf16[7,96,96]{2,1,0:T(8,128)(2,1)} %refs_5_.1, f32[1,96]{1,0:T(1,128)} %bitcast.14, ...), custom_call_target="tpu_custom_call" | custom-call | tf_op jit(solution)/shard_map/voxel_step/pallas_call | solution.py:510
  51.9 0.7 %copy.16 = bf16[96,1024]{1,0:T(8,128)(2,1)} copy(bf16[96,1024]{1,0:T(8,128)(2,1)S(1)} %voxel_step.1) | data formatting | bytes 393216

commit v3 on v2

--- a/solution.py
+++ b/solution.py
@@ -23,11 +23,13 @@
 SHIFTS = (64, -64, 8, -8, 1, -1)
 AWAY = -1e30
 NT_DIMS = (((1,), (1,)), ((), ()))
-QROWS = 256
+SET = 4
 GROUP = 4
 INPUTS = 14
-RUNS = ((0, 3), (4, 5))
-HEAD_ROWS = (slice(0, 32), slice(32, 48))
+WAVES = ((0, 1, 2, 3), (4, 5))
+WAVE_ROWS = (slice(0, 32), slice(32, 48))
+GELU_ONE = math.sqrt(2 / math.pi)
+GELU_THREE = GELU_ONE * 0.044715
 VMEM_LIMIT = 36 * 1024 * 1024
 
 
@@ -85,8 +87,8 @@
         signal,
         taps,
         conv_cat,
+        inside,
         send_pick,
-        remote_pick,
         local_pick,
         spread_pick,
         halo_send,
@@ -105,6 +107,7 @@
         value_rows,
         self_rows,
         heads_out,
+        slot_acc,
         back_send,
         back_recv,
         halo_sems,
@@ -114,8 +117,6 @@
         input_sems,
     ) = refs[2 * INPUTS + 1 :]
     loads = [pltpu.make_async_copy(sources[i], held[i], input_sems.at[i]) for i in range(INPUTS)]
-    for load in loads:
-        load.start()
     (
         feats,
         occupancy,
@@ -143,6 +144,8 @@
         pl.semaphore_signal(
             barrier, inc=1, device_id={"block": lax.rem(me_b + off + nb, nb)}, device_id_type=MESH
         )
+    for load in loads:
+        load.start()
     for k in range(1, nt):
         pl.semaphore_signal(
             barrier, inc=1, device_id={"token": lax.rem(me_t + k, nt)}, device_id_type=MESH
@@ -171,16 +174,16 @@
     label_copy = lambda k: token_copy(label_send, label_recv, label_sems, k, k)
     data_copy = lambda k: token_copy(data_send, data_recv, data_sems, k, k)
 
-    def back_copy(t, k):
+
+    def back_copy(wave, k):
         return pltpu.make_async_remote_copy(
-            src_ref=back_send.at[k, HEAD_ROWS[t]],
-            dst_ref=back_recv.at[k, HEAD_ROWS[t]],
-            send_sem=back_sems.at[0, t, k],
-            recv_sem=back_sems.at[1, t, k],
+            src_ref=back_send.at[k, WAVE_ROWS[wave]],
+            dst_ref=back_recv.at[k, WAVE_ROWS[wave]],
+            send_sem=back_sems.at[0, wave, k],
+            recv_sem=back_sems.at[1, wave, k],
             device_id={"token": lax.rem(me_t - k + nt, nt)},
             device_id_type=MESH,
         )
-
 
     for i in range(4):
         loads[i].wait()
@@ -221,10 +224,11 @@
     for o in range(4):
         halo_copy(0, o).start()
 
+    takes = {}
     for a in range(3):
         for b in range(2):
-            remote_src = jnp.full((1, 128), -1, I32)
             local_src = jnp.full((1, 128), -1, I32)
+            source_of = []
             for side in range(2):
                 f = 2 * a + side
                 own, idx = owner[f, b], index[f, b]
@@ -236,13 +240,15 @@
                         slot = slot + jnp.where(before, 1, 0)
                 gap = me_b - own
                 from_o = jnp.where(gap < 0, gap + 2, gap + 1)
-                remote = (own >= 0) & (gap != 0)
-                base = jnp.where(remote, from_o * 128 + slot * FACE, -4096)
-                remote_src = jnp.where(half == side, within + base, remote_src)
+                source_of.append(jnp.where((own >= 0) & (gap != 0), from_o * 2 + slot, -1))
                 base = jnp.where((own >= 0) & (gap == 0), idx * BLOCK, -4096)
                 local_src = jnp.where(half == side, voxel_of[f ^ 1] + base, local_src)
+            source = jnp.where(half == 0, source_of[0], source_of[1])
+            for o in range(4):
+                for cross in range(2):
+                    hit = source == o * 2 + (half ^ cross)
+                    takes[a, b, o, cross] = jnp.where(hit, 1.0, 0.0).astype(BF16)
             lanes = slice((a * 2 + b) * 128, (a * 2 + b + 1) * 128)
-            store_one_hot(remote_pick, 0, 512, lanes, remote_src)
             store_one_hot(local_pick, 0, rows, lanes, local_src)
     side_row = lax.broadcasted_iota(I32, (128, BLOCK), 0)
     voxel_lane = lax.broadcasted_iota(I32, (128, BLOCK), 1)
@@ -262,26 +268,44 @@
         for f in range(6):
             moved = pltpu.roll(source, SHIFTS[f] % rows, 1) * (1.0 - on_edge[f])
             taps[(f + 1) * channels : (f + 2) * channels, :] = moved.astype(BF16)
-        halo = dot(taps[0:channels, :], local_pick[...])
+        local = dot(taps[0:channels, :], local_pick[...]).astype(BF16)
+        inside[...] = dot(conv_cat[...], taps[...])
         for o in range(4):
             halo_copy(step, o).wait_recv()
-        received = jnp.concatenate([halo_recv[step, o] for o in range(4)], axis=1)
-        halo = (halo + dot(received, remote_pick[...])).astype(BF16)
+        came = [halo_recv[step, o] for o in range(4)]
+        came = [(x, jnp.concatenate([x[:, FACE:], x[:, :FACE]], axis=1)) for x in came]
+
+        def faces(a, b):
+            piece = local[:, (a * 2 + b) * 128 : (a * 2 + b + 1) * 128]
+            for o in range(4):
+                for cross in range(2):
+                    piece = piece + came[o][cross] * takes[a, b, o, cross]
+            return piece
+
+        tiles = [inside[:, c * 128 : (c + 1) * 128] for c in range(rows // 128)]
+        per_block = BLOCK // 128
         for a in range(3):
-            for b in range(2):
-                lanes = slice((a * 2 + b) * 128, (a * 2 + b + 1) * 128)
-                piece = halo[:, lanes]
-                if a == 0:
-                    gap = jnp.zeros((channels, BLOCK - 256), BF16)
-                    wide = jnp.concatenate([piece, gap, piece], axis=1)
-                else:
-                    wide = dot(piece, spread_pick[a - 1]).astype(BF16)
-                cols = slice(b * BLOCK, (b + 1) * BLOCK)
-                for side in range(2):
-                    f = 2 * a + side
-                    tap_rows = slice((f + 1) * channels, (f + 2) * channels)
-                    taps[tap_rows, cols] = taps[tap_rows, cols] + wide * on_edge[f][:, cols].astype(BF16)
-        return dot(conv_cat[...], taps[...])
+            pair = weight[2 * a + 1 : 2 * a + 3].reshape(2 * channels, channels)
+            sides = dot(pair, jnp.concatenate([faces(a, 0), faces(a, 1)], axis=1))
+            edge = [
+                jnp.where(half == 0, sides[:channels, lanes], sides[channels:, lanes])
+                for lanes in (slice(0, 128), slice(128, 256))
+            ]
+            if a == 0:
+                for b in range(2):
+                    first, last = b * per_block, (b + 1) * per_block - 1
+                    tiles[first] = tiles[first] + jnp.where(half == 0, edge[b], 0.0)
+                    tiles[last] = tiles[last] + jnp.where(half == 1, edge[b], 0.0)
+            else:
+                high = [e.astype(BF16) for e in edge]
+                low = [(e - h.astype(F32)).astype(BF16) for e, h in zip(edge, high)]
+                wide = dot(jnp.concatenate(high + low, axis=0), spread_pick[a - 1])
+                for b in range(2):
+                    part = wide[b * channels : (b + 1) * channels] + wide[(b + 2) * channels : (b + 3) * channels]
+                    for c in range(per_block):
+                        t = b * per_block + c
+                        tiles[t] = tiles[t] + part[:, c * 128 : (c + 1) * 128]
+        return jnp.concatenate(tiles, axis=1)
 
     for i in range(4, INPUTS):
         loads[i].wait()
@@ -344,11 +368,10 @@
     block_out[...] = result
     normed = normalise(result.astype(F32), column_of(gain_attn[...])).astype(BF16)
 
-    for g in range(nt // GROUP):
-        ks = order[g * GROUP : (g + 1) * GROUP]
+    for ks in [order[:2], order[2:4]] + [order[g : g + GROUP] for g in range(4, nt, GROUP)]:
         chosen = jnp.concatenate([pack[k * cap : (k + 1) * cap, :] for k in ks], axis=0)
         packed = dot_nt(normed, chosen).astype(BF16)
-        for j, k in enumerate(order[g * GROUP : (g + 1) * GROUP]):
+        for j, k in enumerate(ks):
             part = packed[:, j * cap : (j + 1) * cap]
             if k == 0:
                 data_recv[0] = part
@@ -366,8 +389,8 @@
     query_rows[...] = jnp.zeros_like(query_rows)
     w_out_here = w_out[...].astype(F32).T.astype(BF16)
     w_up_here = w_up[...].astype(F32).T.astype(BF16)
-    for g in range(nt // GROUP):
-        ks = order[g * GROUP : (g + 1) * GROUP]
+    arrivals = [order[g : g + GROUP] for g in range(0, nt - GROUP, GROUP)] + [order[-GROUP:-2], order[-2:]]
+    for g, ks in enumerate(arrivals):
         for k in ks:
             if k:
                 data_copy(k).wait_recv()
@@ -382,6 +405,7 @@
         part = dot_nt(came, chosen)
         serial_acc[...] = part if g == 0 else serial_acc[...] + part
 
+    groups = [order[g * GROUP : (g + 1) * GROUP] for g in range(nt // GROUP)]
     live = serial_acc[channels : channels + 1, :] > 0.5
     width = HEADS * HD
     projected = dot(w_qkv[...], serial_acc[0:channels, :].astype(BF16))
@@ -403,14 +427,18 @@
         query = jnp.concatenate([query_high[own], query_high[own], query_low[own], ones8], axis=0).astype(BF16)
         value_rows[h * 16 : (h + 1) * 16, :] = jnp.concatenate([values[own], ones8], axis=0).astype(BF16)
         for p in range(patches):
-            query_rows[p * HEADS + h, h * 32 : (h + 1) * 32, :] = query[:, p * PATCH : (p + 1) * PATCH]
+            query_rows[p * HEADS + h, h % SET * 32 : (h % SET + 1) * 32, :] = query[:, p * PATCH : (p + 1) * PATCH]
         alone = jnp.sum(scaled[own] * keys[own], axis=0, keepdims=True)
         self_rows[h] = jnp.where(live, AWAY, alone)
-    key_parts.append(jnp.zeros((QROWS - HEADS * 32, rows), F32))
-    key_rows[...] = jnp.concatenate(key_parts, axis=0).T.astype(BF16)
+    key_rows[...] = jnp.concatenate(key_parts, axis=0).astype(BF16).T
 
     def score(p, h):
-        return dot(key_rows[p * PATCH : (p + 1) * PATCH, :], query_rows[p * HEADS + h])
+        first = h // SET * SET
+        last = min(first + SET, HEADS)
+        return dot(
+            key_rows[p * PATCH : (p + 1) * PATCH, first * 32 : last * 32],
+            query_rows[p * HEADS + h, 0 : (last - first) * 32],
+        )
 
     def attend(p, h, scores):
         cols = slice(p * PATCH, (p + 1) * PATCH)
@@ -423,44 +451,60 @@
         top = sums[0:HD] + own * value[0:HD].astype(F32)
         heads_out[h * HD : (h + 1) * HD, cols] = top / (sums[HD : HD + 1] + own)
 
-    def to_slots(heads, p):
-        part = heads_out[heads[0] * HD : (heads[1] + 1) * HD, p * PATCH : (p + 1) * PATCH].astype(BF16)
-        return dot(part, place[p * PATCH : (p + 1) * PATCH, :])
-
-    def give_back(t, slots):
-        slots = slots.astype(BF16)
-        for k in order:
-            part = slots[:, k * cap : (k + 1) * cap]
-            if k == 0:
-                back_recv[0, HEAD_ROWS[t]] = part
-            else:
-                back_send[k, HEAD_ROWS[t]] = part
-        for k in order:
-            if k:
-                back_copy(t, k).start()
-
-    waves = [(t, p) for t in range(len(RUNS)) for p in range(patches)]
-    units = [(t, p, h) for t, p in waves for h in range(RUNS[t][0], RUNS[t][1] + 1)]
+    def to_slots(wave, p, ks):
+        heads = WAVES[wave]
+        part = heads_out[heads[0] * HD : (heads[-1] + 1) * HD, p * PATCH : (p + 1) * PATCH].astype(BF16)
+        chosen = [place[p * PATCH : (p + 1) * PATCH, k * cap : (k + 1) * cap] for k in ks]
+        return dot(part, jnp.concatenate(chosen, axis=1))
+
+    def add_slots(wave, p):
+        for g, ks in enumerate(groups):
+            part = to_slots(wave, p, ks)
+            slot_acc[g, WAVE_ROWS[wave]] = part if p == 0 else slot_acc[g, WAVE_ROWS[wave]] + part
+
+    def give_back(wave, last):
+        for g, ks in enumerate(groups):
+            back = slot_acc[g, WAVE_ROWS[wave]]
+            if last:
+                back = back + to_slots(wave, patches - 1, ks)
+            back = back.astype(BF16)
+            for j, k in enumerate(ks):
+                part = back[:, j * cap : (j + 1) * cap]
+                if k == 0:
+                    back_recv[0, WAVE_ROWS[wave]] = part
+                else:
+                    back_send[k, WAVE_ROWS[wave]] = part
+                    if last:
+                        back_copy(wave, k).start()
+        if not last:
+            for k in order:
+                if k:
+                    back_copy(wave, k).start()
+
+    units = [(wave, p, h) for wave in range(2) for p in range(patches) for h in WAVES[wave]]
     ahead = score(*units[0][1:])
-    slots = None
-    for i, (t, p, h) in enumerate(units):
+    waiting = []
+    for i, (wave, p, h) in enumerate(units):
         scores = ahead
         if i + 1 < len(units):
             ahead = score(*units[i + 1][1:])
         attend(p, h, scores)
-        if h == RUNS[t][1]:
-            part = to_slots(RUNS[t], p)
-            slots = part if p == 0 else slots + part
-            if p == patches - 1:
-                give_back(t, slots)
+        if waiting and h == WAVES[wave][0]:
+            done = waiting.pop()
+            add_slots(*done)
+            if done == (0, patches - 1):
+                give_back(0, False)
+        if h == WAVES[wave][-1]:
+            waiting.append((wave, p))
+    give_back(1, True)
 
     returned = None
     for g in range(nt // GROUP):
         ks = order[g * GROUP : (g + 1) * GROUP]
         for k in ks:
             if k:
-                for t in range(len(RUNS)):
-                    back_copy(t, k).wait_recv()
+                for wave in range(2):
+                    back_copy(wave, k).wait_recv()
         came = jnp.concatenate([back_recv[k] for k in ks], axis=1)
         part = dot(came, jnp.concatenate([pack[k * cap : (k + 1) * cap, :] for k in ks], axis=0))
         returned = part if g == 0 else returned + part
@@ -470,8 +514,9 @@
         cols = slice(c, c + 256)
         combined = block_out[:, cols].astype(F32) + attended[:, cols].astype(F32)
         hidden = dot(w_up_here, normalise(combined, gain).astype(BF16))
-        hidden = jax.nn.gelu(hidden).astype(BF16)
-        summed = combined + dot(w_down[...], hidden)
+        inner = hidden * (GELU_ONE + GELU_THREE * (hidden * hidden))
+        hidden = (hidden + hidden * jnp.tanh(inner)).astype(BF16)
+        summed = combined + 0.5 * dot(w_down[...], hidden)
         out_ref[:, cols] = jnp.where(occupied[:, cols], summed, 0.0).astype(BF16)
 
     for step in range(2):
@@ -480,8 +525,8 @@
     for k in range(1, nt):
         label_copy(k).wait_send()
         data_copy(k).wait_send()
-        for t in range(len(RUNS)):
-            back_copy(t, k).wait_send()
+        for wave in range(2):
+            back_copy(wave, k).wait_send()
 
 
 def per_device(nb, nt, feats, occupancy, adjacency, serial_pos, conv_one, conv_two, gain_one, gain_two, gain_attn, w_qkv, w_out, gain_mlp, w_up, w_down):
@@ -520,8 +565,8 @@
             pltpu.VMEM((channels, rows), BF16),
             pltpu.VMEM((7 * channels, rows), BF16),
             pltpu.VMEM((channels, 7 * channels), BF16),
+            pltpu.VMEM((channels, rows), F32),
             pltpu.VMEM((rows, 512), BF16),
-            pltpu.VMEM((512, 768), BF16),
             pltpu.VMEM((rows, 768), BF16),
             pltpu.VMEM((2, 128, BLOCK), BF16),
             pltpu.VMEM((2, 4, channels, 128), BF16),
@@ -535,17 +580,18 @@
             pltpu.VMEM((nt, channels, cap), BF16),
             pltpu.VMEM((nt, channels, cap), BF16),
             pltpu.VMEM((channels + 16, rows), F32),
-            pltpu.VMEM((rows, QROWS), BF16),
-            pltpu.VMEM((patches * HEADS, QROWS, PATCH), BF16),
+            pltpu.VMEM((rows, HEADS * 32), BF16),
+            pltpu.VMEM((patches * HEADS, SET * 32, PATCH), BF16),
             pltpu.VMEM((HEADS * 16, rows), BF16),
             pltpu.VMEM((HEADS, 1, rows), F32),
             pltpu.VMEM((width, rows), F32),
+            pltpu.VMEM((nt // GROUP, width, GROUP * cap), F32),
             pltpu.VMEM((nt, width, cap), BF16),
             pltpu.VMEM((nt, width, cap), BF16),
             pltpu.SemaphoreType.DMA((2, 2, 4)),
             pltpu.SemaphoreType.DMA((2, nt)),
             pltpu.SemaphoreType.DMA((2, nt)),
-            pltpu.SemaphoreType.DMA((2, len(RUNS), nt)),
+            pltpu.SemaphoreType.DMA((2, 2, nt)),
             pltpu.SemaphoreType.DMA((INPUTS,)),
         ],
         compiler_params=pltpu.CompilerParams(

time: 52.7 us -> 52.6 us (level)
  no operation moved by 1% of the time
where the time goes in v3:
time: 52.6 us; the launch traced here: 52.5 us
  Pallas kernels  51.8 us (98%)
  local copies, waits for them, and re-layouts  0.68 us (1%)
    pallas_call x1, Pallas kernels, per_device(): pl.pallas_call(functools.partial(kernel, nb, nt), out_shape=jax.ShapeDtyp...  51.8 us

profile of v3, /device:TPU:1, one launch (start us, length us, event | category | flops | bytes accessed | tf_op | source)
XLA Modules:
  0.0 52.5 jit_solution(8227025881659236186)
XLA Ops:
  0.0 51.8 %voxel_step.1 = bf16[96,1024]{1,0:T(8,128)(2,1)S(1)} custom-call(bf16[96,1024]{1,0:T(8,128)(2,1)} %refs_0_.1, s32[1,1024]{1,0:T(1,128)} %bitcast.11, s32[2,2,6]{2,1,0:T(2,128)} %bitcast.13, s32[1,1024]{1,0:T(1,128)} %bitcast.12, bf16[7,96,96]{2,1,0:T(8,128)(2,1)} %refs_4_.1, bf16[7,96,96]{2,1,0:T(8,128)(2,1)} %refs_5_.1, f32[1,96]{1,0:T(1,128)} %bitcast.14, ...), custom_call_target="tpu_custom_call" | custom-call | tf_op jit(solution)/shard_map/voxel_step/pallas_call | solution.py:555
  51.8 0.7 %copy.16 = bf16[96,1024]{1,0:T(8,128)(2,1)} copy(bf16[96,1024]{1,0:T(8,128)(2,1)S(1)} %voxel_step.1) | data formatting | bytes 393216

commit v4 on v3

--- a/solution.py
+++ b/solution.py
@@ -24,6 +24,7 @@
 AWAY = -1e30
 NT_DIMS = (((1,), (1,)), ((), ()))
 SET = 4
+QCOLS = 256
 GROUP = 4
 INPUTS = 14
 WAVES = ((0, 1, 2, 3), (4, 5))
@@ -389,7 +390,7 @@
     query_rows[...] = jnp.zeros_like(query_rows)
     w_out_here = w_out[...].astype(F32).T.astype(BF16)
     w_up_here = w_up[...].astype(F32).T.astype(BF16)
-    arrivals = [order[g : g + GROUP] for g in range(0, nt - GROUP, GROUP)] + [order[-GROUP:-2], order[-2:]]
+    arrivals = [order[: nt // 2], order[nt // 2 : 3 * nt // 4], order[3 * nt // 4 :]]
     for g, ks in enumerate(arrivals):
         for k in ks:
             if k:
@@ -432,21 +433,22 @@
         self_rows[h] = jnp.where(live, AWAY, alone)
     key_rows[...] = jnp.concatenate(key_parts, axis=0).astype(BF16).T
 
-    def score(p, h):
+    def score(p, h, q):
         first = h // SET * SET
         last = min(first + SET, HEADS)
         return dot(
             key_rows[p * PATCH : (p + 1) * PATCH, first * 32 : last * 32],
-            query_rows[p * HEADS + h, 0 : (last - first) * 32],
+            query_rows[p * HEADS + h, 0 : (last - first) * 32, q * QCOLS : (q + 1) * QCOLS],
         )
 
-    def attend(p, h, scores):
-        cols = slice(p * PATCH, (p + 1) * PATCH)
+    def attend(p, h, q, scores):
+        keys_of = slice(p * PATCH, (p + 1) * PATCH)
+        cols = slice(p * PATCH + q * QCOLS, p * PATCH + (q + 1) * QCOLS)
         alone = self_rows[h, :, cols]
         largest = jnp.maximum(jnp.max(scores, axis=0, keepdims=True), alone)
         weights = jnp.exp2(scores - largest).astype(BF16)
+        sums = dot(value_rows[h * 16 : (h + 1) * 16, keys_of], weights)
         value = value_rows[h * 16 : (h + 1) * 16, cols]
-        sums = dot(value, weights)
         own = jnp.exp2(alone - largest)
         top = sums[0:HD] + own * value[0:HD].astype(F32)
         heads_out[h * HD : (h + 1) * HD, cols] = top / (sums[HD : HD + 1] + own)
@@ -481,26 +483,26 @@
                 if k:
                     back_copy(wave, k).start()
 
-    units = [(wave, p, h) for wave in range(2) for p in range(patches) for h in WAVES[wave]]
-    ahead = score(*units[0][1:])
+    units = [(wave, p, h, q) for wave in range(2) for p in range(patches) for h in WAVES[wave] for q in range(PATCH // QCOLS)]
+    ahead = [score(*unit[1:]) for unit in units[:4]]
     waiting = []
-    for i, (wave, p, h) in enumerate(units):
-        scores = ahead
-        if i + 1 < len(units):
-            ahead = score(*units[i + 1][1:])
-        attend(p, h, scores)
-        if waiting and h == WAVES[wave][0]:
+    for i, (wave, p, h, q) in enumerate(units):
+        scores = ahead.pop(0)
+        if i + 4 < len(units):
+            ahead.append(score(*units[i + 4][1:]))
+        attend(p, h, q, scores)
+        if waiting and h == WAVES[wave][0] and q == 0:
             done = waiting.pop()
             add_slots(*done)
             if done == (0, patches - 1):
                 give_back(0, False)
-        if h == WAVES[wave][-1]:
+        if h == WAVES[wave][-1] and q == PATCH // QCOLS - 1:
             waiting.append((wave, p))
     give_back(1, True)
 
     returned = None
-    for g in range(nt // GROUP):
-        ks = order[g * GROUP : (g + 1) * GROUP]
+    nearest = order[::-1]
+    for g, ks in enumerate([nearest[: nt // 2], nearest[nt // 2 : 3 * nt // 4], nearest[3 * nt // 4 :]]):
         for k in ks:
             if k:
                 for wave in range(2):

time: 52.6 us -> 52.2 us (level)
  no operation moved by 1% of the time
where the time goes in v4:
time: 52.2 us; the launch traced here: 52.1 us
  Pallas kernels  51.4 us (98%)
  local copies, waits for them, and re-layouts  0.68 us (1%)
    pallas_call x1, Pallas kernels, per_device(): pl.pallas_call(functools.partial(kernel, nb, nt), out_shape=jax.ShapeDtyp...  51.4 us

profile of v4, /device:TPU:1, one launch (start us, length us, event | category | flops | bytes accessed | tf_op | source)
XLA Modules:
  0.0 52.1 jit_solution(11844738612118811905)
XLA Ops:
  0.0 51.4 %voxel_step.1 = bf16[96,1024]{1,0:T(8,128)(2,1)S(1)} custom-call(bf16[96,1024]{1,0:T(8,128)(2,1)} %refs_0_.1, s32[1,1024]{1,0:T(1,128)} %bitcast.11, s32[2,2,6]{2,1,0:T(2,128)} %bitcast.13, s32[1,1024]{1,0:T(1,128)} %bitcast.12, bf16[7,96,96]{2,1,0:T(8,128)(2,1)} %refs_4_.1, bf16[7,96,96]{2,1,0:T(8,128)(2,1)} %refs_5_.1, f32[1,96]{1,0:T(1,128)} %bitcast.14, ...), custom_call_target="tpu_custom_call" | custom-call | tf_op jit(solution)/shard_map/voxel_step/pallas_call | solution.py:557
  51.4 0.7 %copy.16 = bf16[96,1024]{1,0:T(8,128)(2,1)} copy(bf16[96,1024]{1,0:T(8,128)(2,1)S(1)} %voxel_step.1) | data formatting | bytes 393216
